TPU v7x, 32 devices: a whole 2x2x4 slice. The times are simulated.
32 devices in a mesh: dp: 4 (over y, core), ctx: 4 (over z), tp: 2 (over x).
Axes of the slice: x: 2, y: 2, z: 4, core: 2. Of those that a mesh axis runs over, the one named last changes fastest.
Arguments:
- tokens: bfloat16 [8, 640, 512], P('dp', 'ctx'), may hold values from -6 to 6
- cotangent: bfloat16 [8, 640, 512], P('dp', 'ctx'), may hold values from -6 to 6
- routes: int32 [8, 640, 2], P('dp', 'ctx'), may hold values from 0 to 15, as said below
- slot_index: int32 [8, 640, 2], P('dp', 'ctx'), may hold values from 0 to 30, as said below
- token_mask: int32 [8, 640], P('dp', 'ctx'), may hold values from 0 to 1, as said below
- image_mask: int32 [8], P('dp'), may hold values from 0 to 1, as said below
- adapter_set: int32 [8], P('dp'), may hold values from 0 to 3
- first_gain: float32 [512], replicated, may hold values from 0.5 to 1.5
- first_shift: float32 [512], replicated, may hold values from -0.5 to 0.5
- second_gain: float32 [512], replicated, may hold values from 0.5 to 1.5
- second_shift: float32 [512], replicated, may hold values from -0.5 to 0.5
- attend_weight: bfloat16 [512, 3, 512], P('dp', None, 'tp'), may hold values from -0.25 to 0.25
- mixing_weight: bfloat16 [512, 512], P('dp', 'tp'), may hold values from -0.75 to 0.75
- router_weight: bfloat16 [512, 16], P('dp'), may hold values from -0.1875 to 0.1875
- expand_weight: bfloat16 [16, 512, 2048], P('dp', None, 'tp'), may hold values from -0.25 to 0.25
- shrink_weight: bfloat16 [16, 2048, 512], P('dp', 'tp'), may hold values from -2 to 2
- attend_down: bfloat16 [4, 512, 16], replicated, may hold values from -0.25 to 0.25
- attend_up: bfloat16 [4, 16, 3, 512], replicated, may hold values from -0.75 to 0.75
- mixing_down: bfloat16 [4, 512, 16], replicated, may hold values from -0.25 to 0.25
- mixing_up: bfloat16 [4, 16, 512], replicated, may hold values from -1.5 to 1.5
- router_down: bfloat16 [4, 512, 16], replicated, may hold values from -0.25 to 0.25
- router_up: bfloat16 [4, 16, 16], replicated, may hold values from -0.75 to 0.75
- expand_down: bfloat16 [4, 16, 512, 16], replicated, may hold values from -0.25 to 0.25
- expand_up: bfloat16 [4, 16, 16, 2048], replicated, may hold values from -0.75 to 0.75
- shrink_down: bfloat16 [4, 16, 2048, 16], replicated, may hold values from -0.125 to 0.125
- shrink_up: bfloat16 [4, 16, 16, 512], replicated, may hold values from -6 to 6
Outputs:
- layer_out: bfloat16 [8, 640, 512], P('dp', 'ctx')
- tokens_grad: bfloat16 [8, 640, 512], P('dp', 'ctx')
- grad_attend_down: float32 [4, 512, 16], replicated
- grad_attend_up: float32 [4, 16, 3, 512], replicated
- grad_mixing_down: float32 [4, 512, 16], replicated
- grad_mixing_up: float32 [4, 16, 512], replicated
- grad_router_down: float32 [4, 512, 16], replicated
- grad_router_up: float32 [4, 16, 16], replicated
- grad_expand_down: float32 [4, 16, 512, 16], replicated
- grad_expand_up: float32 [4, 16, 16, 2048], replicated
- grad_shrink_down: float32 [4, 16, 2048, 16], replicated
- grad_shrink_up: float32 [4, 16, 16, 512], replicated
Inputs may be any that keep to these rules, and one draw needn't show every extreme that they name: `routes`: each token names two different experts. In every image block of 160 positions the first 31 tokens name one common expert first. `slot_index`: A pair's value is the number of earlier pairs (positions in order, a token's first expert before its second) of the same image block that name the same expert and belong to live tokens; pairs of tokens that are not live and pairs counted 30 or more hold 30, which means dropped. `token_mask`: the real tokens of each image are a prefix of more than half of its 640 positions. `image_mask`: the first image is real, and at least one image is a pad.
All inputs are finite; a program needn't handle non-finite values.
Results may differ from a plain program's by a relative error of at most 0.022.
Values may be sent and summed in bfloat16 or wider, within the bound.
A program may use at most 192 MiB of HBM per device.

v0:
```python
import jax
import jax.numpy as jnp
from jax import lax
from jax.sharding import PartitionSpec as P

D = 512
HEADS = 8
HD = 64
FF = 2048
EXPERTS = 16
TOP = 2
RANK = 16
SETS = 4
CAP = 30


EPSILON = 1e-06
MASKED = -1e30
SQRT_HALF = 0.7071067811865476
INV_ROOT_TWO_PI = 0.3989422804014327
SINGLE_TYPE = jnp.float32
NARROW_TYPE = jnp.bfloat16


def matmul(left_side, right_side):
    return jnp.dot(left_side, right_side, preferred_element_type=SINGLE_TYPE)


def inner_rows(left_side, right_side):
    return lax.dot_general(
        left_side, right_side, (((0,), (0,)), ((), ())), preferred_element_type=SINGLE_TYPE
    )


def times_transposed(left_side, right_side):
    return lax.dot_general(
        left_side, right_side, (((1,), (1,)), ((), ())), preferred_element_type=SINGLE_TYPE
    )


def normalize(values, gain_row, shift_row):
    centred = values - jnp.mean(values, axis=-1, keepdims=True)
    spread = jnp.mean(centred * centred, axis=-1, keepdims=True)
    factor = lax.rsqrt(spread + EPSILON)
    normed = centred * factor
    return (normed * gain_row + shift_row, normed, factor)


def normalize_back(grad_out, normed, factor, gain_row):
    scaled = grad_out * gain_row
    return factor * (
        scaled
        - jnp.mean(scaled, axis=-1, keepdims=True)
        - normed * jnp.mean(scaled * normed, axis=-1, keepdims=True)
    )


def choose(values, set_rows):
    return values * jnp.repeat(set_rows, RANK, axis=-1)


def softmax_rows(values):
    row_top = jnp.max(values, axis=-1, keepdims=True)
    powers = jnp.exp(values - row_top)
    return powers / jnp.sum(powers, axis=-1, keepdims=True)


def gelu_slope(values):
    return 0.5 * (1.0 + lax.erf(values * SQRT_HALF)) + values * INV_ROOT_TWO_PI * jnp.exp(
        -0.5 * values * values
    )


def attend_image(mapped):
    image_queries, image_keys, image_values, image_live = mapped
    key_open = (image_live > 0)[None, None, :]
    scores = jnp.einsum(
        "qhd,khd->hqk", image_queries, image_keys, preferred_element_type=SINGLE_TYPE
    ) * HD ** (-0.5)
    scores = jnp.where(key_open, scores, MASKED)
    row_top = jnp.max(scores, axis=-1, keepdims=True)
    powers = jnp.exp(scores - row_top)
    row_total = jnp.sum(powers, axis=-1, keepdims=True)
    weights_att = (powers / row_total).astype(NARROW_TYPE)
    head_mix = jnp.einsum(
        "hqk,khd->qhd", weights_att, image_values, preferred_element_type=SINGLE_TYPE
    )
    return (head_mix.astype(NARROW_TYPE), row_top, row_total)


def attend_image_back(mapped):
    image_queries, image_keys, image_values, image_live, image_grad, row_top, row_total = mapped
    score_scale = HD ** (-0.5)
    key_open = (image_live > 0)[None, None, :]
    scores_again = (
        jnp.einsum("qhd,khd->hqk", image_queries, image_keys, preferred_element_type=SINGLE_TYPE)
        * score_scale
    )
    probs_again = jnp.exp(jnp.where(key_open, scores_again, MASKED) - row_top) / row_total
    grad_probs_att = jnp.einsum(
        "qhd,khd->hqk", image_grad, image_values, preferred_element_type=SINGLE_TYPE
    )
    grad_scores = (
        probs_again
        * (grad_probs_att - jnp.sum(grad_probs_att * probs_again, axis=-1, keepdims=True))
    ).astype(NARROW_TYPE)
    grad_queries = (
        jnp.einsum("hqk,khd->qhd", grad_scores, image_keys, preferred_element_type=SINGLE_TYPE)
        * score_scale
    )
    grad_keys_all = (
        jnp.einsum("hqk,qhd->khd", grad_scores, image_queries, preferred_element_type=SINGLE_TYPE)
        * score_scale
    )
    grad_values_all = jnp.einsum(
        "hqk,qhd->khd",
        probs_again.astype(NARROW_TYPE),
        image_grad,
        preferred_element_type=SINGLE_TYPE,
    )
    return (grad_queries, grad_keys_all, grad_values_all)


def expert_adapters(
    expand_down, expand_up, shrink_down, shrink_up, start, number, ff_start, ff_count
):
    set_width = SETS * RANK
    first_a = lax.dynamic_slice_in_dim(expand_down, start, number, 1)
    first_a = jnp.transpose(first_a, (1, 2, 0, 3)).reshape(number, D, set_width)
    first_b = lax.dynamic_slice_in_dim(
        lax.dynamic_slice_in_dim(expand_up, start, number, 1), ff_start, ff_count, 3
    )
    first_b = jnp.transpose(first_b, (1, 0, 2, 3)).reshape(number, set_width, ff_count)
    second_a = lax.dynamic_slice_in_dim(
        lax.dynamic_slice_in_dim(shrink_down, start, number, 1), ff_start, ff_count, 2
    )
    second_a = jnp.transpose(second_a, (1, 2, 0, 3)).reshape(number, ff_count, set_width)
    second_b = lax.dynamic_slice_in_dim(shrink_up, start, number, 1)
    second_b = jnp.transpose(second_b, (1, 0, 2, 3)).reshape(number, set_width, D)
    return (first_a, first_b, second_a, second_b)


def expert_forward(rows_in, set_values, up_weight, down_weight, adapters_local):
    first_a, first_b, second_a, second_b = adapters_local
    set_rows = (
        set_values.astype(SINGLE_TYPE)[..., None] == jnp.arange(SETS).astype(SINGLE_TYPE)
    ).astype(SINGLE_TYPE)
    picker = jnp.repeat(set_rows, RANK, axis=-1)[:, :, None, :]
    lifted = (
        jnp.einsum("secd,edr->secr", rows_in, first_a, preferred_element_type=SINGLE_TYPE) * picker
    ).astype(NARROW_TYPE)
    before = jnp.einsum(
        "secd,edf->secf", rows_in, up_weight, preferred_element_type=SINGLE_TYPE
    ) + jnp.einsum("secr,erf->secf", lifted, first_b, preferred_element_type=SINGLE_TYPE)
    active = jax.nn.gelu(before, approximate=False).astype(NARROW_TYPE)
    partial_out = jnp.einsum(
        "secf,efd->secd", active, down_weight, preferred_element_type=SINGLE_TYPE
    )
    partial_low = jnp.einsum("secf,efr->secr", active, second_a, preferred_element_type=SINGLE_TYPE)
    summed_out, summed_low = (
        lax.psum(partial_out.astype(jnp.bfloat16), "tp").astype(jnp.float32),
        lax.psum(partial_low.astype(jnp.bfloat16), "tp").astype(jnp.float32),
    )
    lowered = (summed_low * picker).astype(NARROW_TYPE)
    result = (
        summed_out
        + jnp.einsum("secr,erd->secd", lowered, second_b, preferred_element_type=SINGLE_TYPE)
    ).astype(NARROW_TYPE)
    return (result, (rows_in, picker, lifted, before, active, lowered))


def expert_backward(grad_out, kept_values, up_weight, down_weight, adapters_local, first_rank):
    rows_in, picker, lifted, before, active, lowered = kept_values
    first_a, first_b, second_a, second_b = adapters_local
    grad_second_b = (
        jnp.einsum("secr,secd->erd", lowered, grad_out, preferred_element_type=SINGLE_TYPE)
        * first_rank
    )
    grad_lowered = (
        jnp.einsum("secd,erd->secr", grad_out, second_b, preferred_element_type=SINGLE_TYPE)
        * picker
    ).astype(NARROW_TYPE)
    grad_second_a = jnp.einsum(
        "secf,secr->efr", active, grad_lowered, preferred_element_type=SINGLE_TYPE
    )
    grad_active = jnp.einsum(
        "secd,efd->secf", grad_out, down_weight, preferred_element_type=SINGLE_TYPE
    ) + jnp.einsum("secr,efr->secf", grad_lowered, second_a, preferred_element_type=SINGLE_TYPE)
    grad_before = (grad_active * gelu_slope(before)).astype(NARROW_TYPE)
    grad_first_b = jnp.einsum(
        "secr,secf->erf", lifted, grad_before, preferred_element_type=SINGLE_TYPE
    )
    partial_rows = jnp.einsum(
        "secf,edf->secd", grad_before, up_weight, preferred_element_type=SINGLE_TYPE
    )
    partial_lift = jnp.einsum(
        "secf,erf->secr", grad_before, first_b, preferred_element_type=SINGLE_TYPE
    )
    summed_rows, summed_lift = (
        lax.psum(partial_rows.astype(jnp.bfloat16), "tp").astype(jnp.float32),
        lax.psum(partial_lift.astype(jnp.bfloat16), "tp").astype(jnp.float32),
    )
    grad_lifted = (summed_lift * picker).astype(NARROW_TYPE)
    grad_first_a = (
        jnp.einsum("secd,secr->edr", rows_in, grad_lifted, preferred_element_type=SINGLE_TYPE)
        * first_rank
    )
    grad_rows = (
        summed_rows
        + jnp.einsum("secr,edr->secd", grad_lifted, first_a, preferred_element_type=SINGLE_TYPE)
    ).astype(NARROW_TYPE)
    return (grad_rows, (grad_first_a, grad_first_b, grad_second_a, grad_second_b))


def place_expert_grads(expert_grads, start, ff_start):
    grad_first_a, grad_first_b, grad_second_a, grad_second_b = expert_grads
    number = grad_first_a.shape[0]
    ff_count = grad_first_b.shape[2]
    first_a = jnp.transpose(grad_first_a.reshape(number, D, SETS, RANK), (2, 0, 1, 3))
    full_first_a = lax.dynamic_update_slice(
        jnp.zeros((SETS, EXPERTS, D, RANK), SINGLE_TYPE), first_a, (0, start, 0, 0)
    )
    first_b = jnp.transpose(grad_first_b.reshape(number, SETS, RANK, ff_count), (1, 0, 2, 3))
    full_first_b = lax.dynamic_update_slice(
        jnp.zeros((SETS, EXPERTS, RANK, FF), SINGLE_TYPE), first_b, (0, start, 0, ff_start)
    )
    second_a = jnp.transpose(grad_second_a.reshape(number, ff_count, SETS, RANK), (2, 0, 1, 3))
    full_second_a = lax.dynamic_update_slice(
        jnp.zeros((SETS, EXPERTS, FF, RANK), SINGLE_TYPE), second_a, (0, start, ff_start, 0)
    )
    second_b = jnp.transpose(grad_second_b.reshape(number, SETS, RANK, D), (1, 0, 2, 3))
    full_second_b = lax.dynamic_update_slice(
        jnp.zeros((SETS, EXPERTS, RANK, D), SINGLE_TYPE), second_b, (0, start, 0, 0)
    )
    return (full_first_a, full_first_b, full_second_a, full_second_b)


def per_device(
    tokens,
    cotangent,
    routes,
    slot_index,
    token_mask,
    image_mask,
    adapter_set,
    first_gain,
    first_shift,
    second_gain,
    second_shift,
    attend_weight,
    mixing_weight,
    router_weight,
    expand_weight,
    shrink_weight,
    attend_down,
    attend_up,
    mixing_down,
    mixing_up,
    router_down,
    router_up,
    expand_down,
    expand_up,
    shrink_down,
    shrink_up,
):
    image_count = tokens.shape[0]
    block_tokens = tokens.shape[1]
    token_count = image_count * block_tokens
    lane_count = attend_weight.shape[2]
    local_heads = lane_count // HD
    hidden_half = expand_weight.shape[2]
    local_experts = expand_weight.shape[0]
    tensor_index = lax.axis_index("tp")
    data_index = lax.axis_index("dp")
    first_rank = (tensor_index == 0).astype(SINGLE_TYPE)
    ff_start = tensor_index * hidden_half
    lane_start = tensor_index * lane_count
    owned_start = data_index * local_experts
    set_width = SETS * RANK
    attend_full, mixing_full, router_full = (
        lax.all_gather(attend_weight, "dp", axis=0, tiled=True),
        lax.all_gather(mixing_weight, "dp", axis=0, tiled=True),
        lax.all_gather(router_weight, "dp", axis=0, tiled=True),
    )
    attend_matrix = attend_full.reshape(D, 3 * lane_count)
    attend_low = jnp.transpose(attend_down, (1, 0, 2)).reshape(D, set_width)
    attend_high = lax.dynamic_slice_in_dim(attend_up, lane_start, lane_count, 3).reshape(
        set_width, 3 * lane_count
    )
    mixing_low = jnp.transpose(
        lax.dynamic_slice_in_dim(mixing_down, lane_start, lane_count, 1), (1, 0, 2)
    ).reshape(lane_count, set_width)
    mixing_high = mixing_up.reshape(set_width, D)
    router_low = jnp.transpose(router_down, (1, 0, 2)).reshape(D, set_width)
    router_high = router_up.reshape(set_width, EXPERTS)
    live_rows = (token_mask * image_mask[:, None]).astype(SINGLE_TYPE)
    set_hot = (adapter_set[:, None] == jnp.arange(SETS)[None, :]).astype(SINGLE_TYPE)
    token_sets = jnp.repeat(set_hot, block_tokens, axis=0)
    flat_in = tokens.reshape(token_count, D).astype(SINGLE_TYPE)
    normed_one, unit_one, factor_one = normalize(flat_in, first_gain, first_shift)
    attend_in = normed_one.astype(NARROW_TYPE)
    attend_lift = choose(matmul(attend_in, attend_low), token_sets).astype(NARROW_TYPE)
    joined_rows = matmul(attend_in, attend_matrix) + matmul(attend_lift, attend_high)
    joined_rows = joined_rows.astype(NARROW_TYPE).reshape(
        image_count, block_tokens, 3, local_heads, HD
    )
    queries = joined_rows[:, :, 0]
    key_block = joined_rows[:, :, 1]
    value_block = joined_rows[:, :, 2]
    all_keys, all_values, all_live = (
        lax.all_gather(key_block, "ctx", axis=1, tiled=True),
        lax.all_gather(value_block, "ctx", axis=1, tiled=True),
        lax.all_gather(live_rows.astype(NARROW_TYPE), "ctx", axis=1, tiled=True),
    )
    head_mix, row_tops, row_totals = lax.map(
        attend_image, (queries, all_keys, all_values, all_live)
    )
    head_mix = head_mix.reshape(token_count, lane_count)
    partial_mix = times_transposed(head_mix, mixing_full)
    partial_lift = matmul(head_mix, mixing_low)
    summed_mix, summed_lift = lax.psum((partial_mix, partial_lift), "tp")
    mixing_lift = choose(summed_lift, token_sets).astype(NARROW_TYPE)
    hidden = flat_in + summed_mix + matmul(mixing_lift, mixing_high)
    normed_two, unit_two, factor_two = normalize(hidden, second_gain, second_shift)
    expert_in = normed_two.astype(NARROW_TYPE)
    router_lift = choose(matmul(expert_in, router_low), token_sets).astype(NARROW_TYPE)
    logits = matmul(expert_in, router_full) + matmul(router_lift, router_high)
    gate_probs = softmax_rows(logits)
    route_hot = (routes.reshape(token_count, TOP)[..., None] == jnp.arange(EXPERTS)).astype(
        SINGLE_TYPE
    )
    gate_values = jnp.sum(gate_probs[:, None, :] * route_hot, axis=-1)
    targets = jnp.where(slot_index < CAP, routes * CAP + slot_index, -1)
    slot_table = (targets[..., None] == jnp.arange(EXPERTS * CAP)).astype(NARROW_TYPE)
    send_rows = jnp.einsum(
        "itks,itd->isd",
        slot_table,
        expert_in.reshape(image_count, block_tokens, D),
        preferred_element_type=SINGLE_TYPE,
    )
    send_rows = send_rows.astype(NARROW_TYPE).reshape(image_count, EXPERTS, CAP, D)
    set_values = jnp.broadcast_to(adapter_set.astype(NARROW_TYPE)[:, None], (image_count, EXPERTS))
    local_adapters = expert_adapters(
        expand_down,
        expand_up,
        shrink_down,
        shrink_up,
        owned_start,
        local_experts,
        ff_start,
        hidden_half,
    )
    up_used, down_used = (expand_weight, shrink_weight)
    recv_rows, recv_sets = (
        lax.all_to_all(send_rows, "dp", split_axis=1, concat_axis=0, tiled=True),
        lax.all_to_all(set_values, "dp", split_axis=1, concat_axis=0, tiled=True),
    )
    out_rows, expert_kept = expert_forward(recv_rows, recv_sets, up_used, down_used, local_adapters)
    back_rows = lax.all_to_all(out_rows, "dp", split_axis=0, concat_axis=1, tiled=True)
    returned = jnp.einsum(
        "itks,isd->itkd",
        slot_table,
        back_rows.reshape(image_count, EXPERTS * CAP, D),
        preferred_element_type=SINGLE_TYPE,
    )
    returned = returned.reshape(token_count, TOP, D)
    output = hidden + jnp.sum(gate_values[..., None] * returned, axis=1)
    layer_out = output.astype(NARROW_TYPE).reshape(image_count, block_tokens, D)
    grad_output = cotangent.reshape(token_count, D).astype(SINGLE_TYPE) * live_rows.reshape(
        token_count, 1
    )
    grad_gates = jnp.sum(grad_output[:, None, :] * returned, axis=-1)
    grad_returned = (gate_values[..., None] * grad_output[:, None, :]).astype(NARROW_TYPE)
    grad_send = jnp.einsum(
        "itks,itkd->isd",
        slot_table,
        grad_returned.reshape(image_count, block_tokens, TOP, D),
        preferred_element_type=SINGLE_TYPE,
    )
    grad_send = grad_send.astype(NARROW_TYPE).reshape(image_count, EXPERTS, CAP, D)
    grad_recv = lax.all_to_all(grad_send, "dp", split_axis=1, concat_axis=0, tiled=True)
    grad_rows, expert_grads = expert_backward(
        grad_recv, expert_kept, up_used, down_used, local_adapters, first_rank
    )
    grad_back = lax.all_to_all(grad_rows, "dp", split_axis=0, concat_axis=1, tiled=True)
    grad_from_experts = jnp.einsum(
        "itks,isd->itd",
        slot_table,
        grad_back.reshape(image_count, EXPERTS * CAP, D),
        preferred_element_type=SINGLE_TYPE,
    )
    grad_from_experts = grad_from_experts.reshape(token_count, D)
    grad_probs = jnp.sum(grad_gates[..., None] * route_hot, axis=1)
    grad_logits = (
        gate_probs * (grad_probs - jnp.sum(grad_probs * gate_probs, axis=-1, keepdims=True))
    ).astype(NARROW_TYPE)
    grad_router_high = inner_rows(router_lift, grad_logits) * first_rank
    grad_router_lift = choose(times_transposed(grad_logits, router_high), token_sets).astype(
        NARROW_TYPE
    )
    grad_router_low = inner_rows(expert_in, grad_router_lift) * first_rank
    grad_expert_in = (
        grad_from_experts
        + times_transposed(grad_logits, router_full)
        + times_transposed(grad_router_lift, router_low)
    )
    grad_hidden = grad_output + normalize_back(grad_expert_in, unit_two, factor_two, second_gain)
    grad_attended = grad_hidden.astype(NARROW_TYPE)
    grad_mixing_high = inner_rows(mixing_lift, grad_attended) * first_rank
    grad_mixing_lift = choose(times_transposed(grad_attended, mixing_high), token_sets).astype(
        NARROW_TYPE
    )
    grad_mixing_low = inner_rows(head_mix, grad_mixing_lift)
    grad_heads = matmul(grad_attended, mixing_full) + times_transposed(grad_mixing_lift, mixing_low)
    grad_heads = grad_heads.astype(NARROW_TYPE).reshape(image_count, block_tokens, local_heads, HD)
    grad_queries, grad_keys_all, grad_values_all = lax.map(
        attend_image_back,
        (queries, all_keys, all_values, all_live, grad_heads, row_tops, row_totals),
    )
    grad_keys, grad_values = (
        lax.psum_scatter(
            grad_keys_all.astype(jnp.bfloat16), "ctx", scatter_dimension=1, tiled=True
        ).astype(jnp.float32),
        lax.psum_scatter(
            grad_values_all.astype(jnp.bfloat16), "ctx", scatter_dimension=1, tiled=True
        ).astype(jnp.float32),
    )
    grad_joined = (
        jnp.stack([grad_queries, grad_keys, grad_values], axis=2)
        .astype(NARROW_TYPE)
        .reshape(token_count, 3 * lane_count)
    )
    grad_attend_high = inner_rows(attend_lift, grad_joined)
    partial_in = times_transposed(grad_joined, attend_matrix)
    partial_up = times_transposed(grad_joined, attend_high)
    summed_in, summed_up = (
        lax.psum(partial_in.astype(jnp.bfloat16), "tp").astype(jnp.float32),
        lax.psum(partial_up.astype(jnp.bfloat16), "tp").astype(jnp.float32),
    )
    grad_attend_lift = choose(summed_up, token_sets).astype(NARROW_TYPE)
    grad_attend_low = inner_rows(attend_in, grad_attend_lift) * first_rank
    grad_attend_in = summed_in + times_transposed(grad_attend_lift, attend_low)
    grad_tokens = grad_hidden + normalize_back(grad_attend_in, unit_one, factor_one, first_gain)
    tokens_grad = grad_tokens.astype(NARROW_TYPE).reshape(image_count, block_tokens, D)
    full_attend_down = jnp.transpose(grad_attend_low.reshape(D, SETS, RANK), (1, 0, 2))
    full_attend_up = lax.dynamic_update_slice(
        jnp.zeros((SETS, RANK, 3, HEADS * HD), SINGLE_TYPE),
        grad_attend_high.reshape(SETS, RANK, 3, lane_count),
        (0, 0, 0, lane_start),
    )
    mixing_rows = jnp.transpose(grad_mixing_low.reshape(lane_count, SETS, RANK), (1, 0, 2))
    full_mixing_down = lax.dynamic_update_slice(
        jnp.zeros((SETS, HEADS * HD, RANK), SINGLE_TYPE), mixing_rows, (0, lane_start, 0)
    )
    full_mixing_up = grad_mixing_high.reshape(SETS, RANK, D)
    full_router_down = jnp.transpose(grad_router_low.reshape(D, SETS, RANK), (1, 0, 2))
    full_router_up = grad_router_high.reshape(SETS, RANK, EXPERTS)
    full_first_a, full_first_b, full_second_a, full_second_b = place_expert_grads(
        expert_grads, owned_start, ff_start
    )
    reduced = lax.psum(
        (
            full_attend_down,
            full_attend_up,
            full_mixing_down,
            full_mixing_up,
            full_router_down,
            full_router_up,
            full_first_a,
            full_first_b,
            full_second_a,
            full_second_b,
        ),
        ("dp", "ctx", "tp"),
    )
    return (
        layer_out,
        tokens_grad,
        reduced[0],
        reduced[1],
        reduced[2],
        reduced[3],
        reduced[4],
        reduced[5],
        reduced[6],
        reduced[7],
        reduced[8],
        reduced[9],
    )


def solution(mesh):
    in_specs = (
        P("dp", "ctx", None),
        P("dp", "ctx", None),
        P("dp", "ctx", None),
        P("dp", "ctx", None),
        P("dp", "ctx"),
        P("dp"),
        P("dp"),
        P(),
        P(),
        P(),
        P(),
        P("dp", None, "tp"),
        P("dp", "tp"),
        P("dp", None),
        P("dp", None, "tp"),
        P("dp", "tp", None),
        P(),
        P(),
        P(),
        P(),
        P(),
        P(),
        P(),
        P(),
        P(),
        P(),
    )
    out_specs = (
        P("dp", "ctx", None),
        P("dp", "ctx", None),
        P(),
        P(),
        P(),
        P(),
        P(),
        P(),
        P(),
        P(),
        P(),
        P(),
    )
    return jax.shard_map(
        per_device, mesh=mesh, in_specs=in_specs, out_specs=out_specs, check_vma=False
    )
```

profile of v0, /device:TPU:1, one launch (start us, length us, event | category | flops | bytes accessed | tf_op | source)
XLA Modules:
  0.0 845.2 jit_solution(5583545326244088726)
XLA Ops:
  11.2 10.0 %all-gather.2 = bf16[4,160,2]{1,2,0:T(2,128)(2,1)S(1)} all-gather(bf16[1,160,2]{1,2,0:T(2,128)(2,1)S(1)} %get-tuple-element.267), channel_id=1, replica_groups=mesh['dp'=4,'ctx'=4,'tp'=2] {'ctx'}, dimensions={0}, use_global_device_ids=true | all-gather | bytes 3200 | tf_op jit(solution)/shard_map/all_gather | solution.py:313
  24.3 9.9 %all_gather.22 = bf16[512,256]{1,0:T(8,128)(2,1)} all-gather(bf16[128,256]{1,0:T(8,128)(2,1)} %param.42), channel_id=1, replica_groups=mesh['dp'=4,'ctx'=4,'tp'=2] {'dp'}, dimensions={0}, use_global_device_ids=true | all-gather | bytes 327680 | tf_op jit(solution)/shard_map/all_gather | solution.py:282
  34.2 8.7 %all_gather.18 = bf16[512,3,256]{0,2,1:T(8,128)(2,1)S(1)} all-gather(bf16[128,3,256]{0,2,1:T(8,128)(2,1)S(1)} %copy.181), channel_id=1, replica_groups=mesh['dp'=4,'ctx'=4,'tp'=2] {'dp'}, dimensions={0}, use_global_device_ids=true | all-gather | bytes 983040 | tf_op jit(solution)/shard_map/all_gather | solution.py:281
  48.8 24.5 %all-gather = bf16[2,640,1,4,64]{4,3,2,0,1:T(4,128)(2,1)S(1)} all-gather(bf16[2,160,1,4,64]{4,3,2,0,1:T(4,128)(2,1)S(1)} %copy.184), channel_id=2, replica_groups=mesh['dp'=4,'ctx'=4,'tp'=2] {'ctx'}, dimensions={1}, use_global_device_ids=true | all-gather | bytes 819200 | tf_op jit(solution)/shard_map/all_gather | solution.py:312
  73.3 2.5 copy.187
  75.8 22.8 %all-gather.1 = bf16[2,640,1,4,64]{4,3,2,0,1:T(4,128)(2,1)S(1)} all-gather(bf16[2,160,1,4,64]{4,3,2,0,1:T(4,128)(2,1)S(1)} %copy.186), channel_id=3, replica_groups=mesh['dp'=4,'ctx'=4,'tp'=2] {'ctx'}, dimensions={1}, use_global_device_ids=true | all-gather | bytes 819200 | tf_op jit(solution)/shard_map/all_gather | solution.py:311
  98.6 1.6 copy.189
  100.2 7.0 while.28
  101.4 2.3 fusion.224
  104.9 2.3 fusion.224
  111.4 6.6 all-to-all-start.1
  118.2 5.1 all_gather.23
  124.3 21.9 %all-reduce.12.cloned.1.call-done = (f32[320,512]{1,0:T(8,128)}, f32[320,64]{0,1:T(8,128)}) async-done(((f32[320,512]{1,0:T(8,128)}, f32[320,64]{0,1:T(8,128)}), (f32[320,512]{1,0:T(8,128)}, f32[320,64]{0,1:T(8,128)})) %all-reduce.12.cloned.1.call-update) | async-done | bytes 737296 | tf_op jit(solution)/shard_map/psum | solution.py:321
  147.2 2.1 fusion.104
  151.9 2.1 bitcast_convert_fusion
  154.0 2.0 copy.203
  156.0 5.1 all-to-all-start.3
  161.9 2.0 copy.193
  163.8 10.2 %all-to-all-done.3 = bf16[2,16,30,512]{3,0,2,1:T(2,128)(2,1)} async-done(((bf16[2,16,30,512]{3,0,2,1:T(2,128)(2,1)}), bf16[2,16,30,512]{3,0,2,1:T(2,128)(2,1)}, u32[]{:S(2)}, u32[]{:S(2)}) %all-to-all-start.3) | async-done | bytes 983072 | tf_op jit(solution)/shard_map/all_to_all | solution.py:381
  174.0 5.1 all-to-all-start
  187.6 4.5 all-to-all-done
  193.5 3.6 fusion.47
  199.4 11.4 %fusion.39 = (bf16[8,4,30,1024]{3,2,0,1:T(8,128)(2,1)S(1)}, f32[8,4,30,1024]{3,2,0,1:T(8,128)S(1)}) fusion(bf16[4,64,1024,1]{2,1,3,0:T(8,128)(2,1)S(1)} %bitcast.463, bf16[8,4,30,64]{3,2,0,1:T(8,128)(2,1)S(1)} %fusion.83, f32[4,8,30,1024]{3,2,1,0:T(8,128)S(1)} %fusion.47), kind=kOutput, calls=%fused_computation.58 | convolution fusion | flops 190709760 | bytes 10477568 | tf_op jit(solution)/shard_map/secr,erf->secf/dot_general | solution.py:154
  210.8 2.2 fusion.71
  214.5 2.1 fusion.44
  218.0 2.3 fusion.68
  220.3 74.3 %all-reduce.14.cloned.1.call-done = (bf16[8,4,30,512]{3,2,0,1:T(8,128)(2,1)}, bf16[8,4,30,64]{3,2,0,1:T(8,128)(2,1)}, bf16[8,4,30,512]{3,2,0,1:T(8,128)(2,1)}, bf16[8,4,30,64]{3,2,0,1:T(8,128)(2,1)}) async-done(((bf16[8,4,30,512]{3,2,0,1:T(8,128)(2,1)}, bf16[8,4,30,64]{3,2,0,1:T(8,128)(2,1)}, bf16[8,4,30,512]{3,2,0,1:T(8,128)(2,1)}, bf16[8,4,30,64]{3,2,0,1:T(8,128)(2,1)}), ...) | async-done | bytes 2211856 | tf_op jit(solution)/shard_map/psum | solution.py:161
  294.6 1.8 fusion.61
  296.4 1.7 copy.200
  298.1 5.1 all-to-all-start.2
  303.2 1.8 fusion.60
  305.0 1.7 copy.205
  306.8 9.4 %all-to-all-done.2 = bf16[8,4,30,512]{3,1,2,0:T(4,128)(2,1)} async-done(((bf16[8,4,30,512]{3,1,2,0:T(4,128)(2,1)}), bf16[8,4,30,512]{3,1,2,0:T(4,128)(2,1)}, u32[]{:S(2)}, u32[]{:S(2)}) %all-to-all-start.2) | async-done | bytes 983072 | tf_op jit(solution)/shard_map/all_to_all | solution.py:359
  316.2 5.1 all-to-all-start.4
  322.6 2.0 copy.201
  324.6 2.7 multiply_reduce_fusion.1
  329.2 5.1 all-to-all-done.4
  334.3 2.1 copy.206
  342.3 1.7 fusion.96
  345.5 12.0 %while.29 = (s32[]{:T(128)}, bf16[2,160,4,64]{1,3,2,0:T(8,128)(2,1)}, bf16[2,640,4,64]{1,3,2,0:T(8,128)(2,1)}, bf16[2,640,4,64]{1,3,2,0:T(8,128)(2,1)}, bf16[2,6...) while((s32[]{:T(128)}, ...), condition=%wide.region_26.27_spmd, body=%wide.region_24.26_spmd.sunk | while | flops 266446080 | bytes 27753672 | solution.py:416
  347.5 1.8 multiply_reduce_fusion.8
  351.6 1.5 exponential_divide_fusion.2
  353.5 1.8 multiply_reduce_fusion.8
  357.6 3.4 copy.246
  360.9 3.4 reshape.397
  364.6 2.1 fusion.130
  368.9 4.9 broadcast_in_dim.137
  375.7 1.6 copy.244
  377.3 1.6 reshape.395
  379.0 1.6 broadcast_in_dim.138
  382.8 1.6 broadcast_in_dim.135
  388.6 18.4 %reduce-scatter.7.cloned.1.call-done = bf16[160,512]{1,0:T(8,128)(2,1)} async-done(((bf16[640,512]{1,0:T(8,128)(2,1)}), bf16[160,512]{1,0:T(8,128)(2,1)}) %reduce-scatter.7.cloned.1.call-update) | async-done | bytes 163856
  409.9 2.3 convolution_convert_fusion.2
  412.9 6.5 psum.133
  421.3 43.3 %psum.139 = f32[4,16,16]{2,1,0:T(8,128)} all-reduce(f32[4,16,16]{2,1,0:T(8,128)S(1)} %bitcast.494), channel_id=1, replica_groups=mesh['dp'=4,'ctx'=4,'tp'=2] {'dp','ctx','tp'}, use_global_device_ids=true, to_apply=%region_38.39 | all-reduce | flops 1024 | bytes 8192 | tf_op jit(solution)/shard_map/psum | solution.py:461
  467.1 346.1 %all-reduce.10.cloned.1.call-done = (f32[4,512,16]{1,2,0:T(8,128)}, f32[4,16,3,512]{3,1,2,0:T(8,128)}, f32[4,512,16]{1,2,0:T(8,128)}, f32[4,16,512]{2,1,0:T(8,12...) async-done(((f32[4,512,16]{1,2,0:T(8,128)}, ...) | async-done | bytes 21889040 | tf_op jit(solution)/shard_map/psum | solution.py:461
  813.2 1.6 copy.312
  814.8 1.8 copy.313
  816.6 1.6 copy.314
  818.1 1.6 copy.315
  819.7 1.6 copy.316
  821.3 3.4 copy.317
  824.6 8.0 copy.318
  832.7 3.9 copy.319
  (373 shorter events, 76.6 us)
Async XLA Ops:
  7.2 171.9 %copy-start = (bf16[4,16,512,16]{2,3,1,0:T(8,128)(2,1)S(1)}, bf16[4,16,512,16]{2,3,1,0:T(8,128)(2,1)}, u32[]{:S(2)}) copy-start(bf16[4,16,512,16]{2,3,1,0:T(8,128)(2,1)} %param.52) | copy-start | bytes 3145732
  7.2 37.7 %copy-start.63 = (bf16[4,512,16]{1,2,0:T(8,128)(2,1)S(1)}, bf16[4,512,16]{1,2,0:T(8,128)(2,1)}, u32[]{:S(2)}) copy-start(bf16[4,512,16]{1,2,0:T(8,128)(2,1)} %param.46) | copy-start | bytes 196612
  7.2 139.0 %all-reduce.12.cloned.1.call-start = ((), (), s32[]{:S(2)}) async-start(), calls=%async_computation.11 | async-start | bytes 1507328 | tf_op jit(solution)/shard_map/psum | solution.py:321
  11.2 112.2 %copy-start.80 = (f32[2,160]{1,0:T(2,128)}, f32[2,160]{1,0:T(2,128)S(1)}, u32[]{:S(2)}) copy-start(f32[2,160]{1,0:T(2,128)S(1)} %get-tuple-element.268) | copy-start | bytes 3844
  21.4 124.8 %copy-start.69 = (f32[320,4]{0,1:T(4,128)}, f32[320,4]{0,1:T(4,128)S(1)}, u32[]{:S(2)}) copy-start(f32[320,4]{0,1:T(4,128)S(1)} %reshape.340) | copy-start | bytes 15364
  22.2 86.6 %copy-start.55 = (bf16[4,256,16]{1,2,0:T(8,128)(2,1)}, bf16[4,256,16]{1,2,0:T(8,128)(2,1)S(1)}, u32[]{:S(2)}) copy-start(bf16[4,256,16]{1,2,0:T(8,128)(2,1)S(1)} %constant_dynamic-slice_fusion.1) | copy-start | bytes 98308
  23.2 21.9 %copy-start.36 = (bf16[8,8,3,256]{3,1,2,0:T(8,128)(2,1)}, bf16[8,8,3,256]{3,1,2,0:T(8,128)(2,1)S(1)}, u32[]{:S(2)}) copy-start(bf16[8,8,3,256]{3,1,2,0:T(8,128)(2,1)S(1)} %copy.248) | copy-start | bytes 294916
  100.2 9.4 %copy-start.23 = (bf16[512,256]{1,0:T(8,128)(2,1)S(1)}, bf16[512,256]{1,0:T(8,128)(2,1)}, u32[]{:S(2)}) copy-start(bf16[512,256]{1,0:T(8,128)(2,1)} %all_gather.22) | copy-start | bytes 786436
  100.2 10.6 %copy-start.94 = (s32[2]{0:T(128)S(1)}, s32[2]{0:T(128)}, u32[]{:S(2)}) copy-start(s32[2]{0:T(128)} %param.36) | copy-start | bytes 28
  100.2 17.9 %copy-start.86 = (s32[2,160,2]{1,2,0:T(2,128)S(1)}, s32[2,160,2]{1,2,0:T(2,128)}, u32[]{:S(2)}) copy-start(s32[2,160,2]{1,2,0:T(2,128)} %param.32) | copy-start | bytes 7684
  100.2 18.0 %copy-start.90 = (bf16[128,16]{0,1:T(8,128)(2,1)S(1)}, bf16[128,16]{0,1:T(8,128)(2,1)}, u32[]{:S(2)}) copy-start(bf16[128,16]{0,1:T(8,128)(2,1)} %param.43) | copy-start | bytes 12292
  100.2 23.1 %copy-start.91 = (s32[2,160,2]{1,2,0:T(2,128)S(1)}, s32[2,160,2]{1,2,0:T(2,128)}, u32[]{:S(2)}) copy-start(s32[2,160,2]{1,2,0:T(2,128)} %param.33) | copy-start | bytes 7684
  100.2 23.1 %copy-start.29 = (bf16[2,160,512]{2,1,0:T(8,128)(2,1)S(1)}, bf16[2,160,512]{2,1,0:T(8,128)(2,1)}, u32[]{:S(2)}) copy-start(bf16[2,160,512]{2,1,0:T(8,128)(2,1)} %param.31) | copy-start | bytes 983044
  107.2 10.9 %copy-start.72 = (f32[2,4,160,1]{2,1,3,0:T(4,128)}, f32[2,4,160,1]{2,1,3,0:T(4,128)S(1)}, u32[]{:S(2)}) copy-start(f32[2,4,160,1]{2,1,3,0:T(4,128)S(1)} %get-tuple-element.461) | copy-start | bytes 15364
  107.2 42.1 %copy-start.74 = (f32[2,4,160,1]{2,1,3,0:T(4,128)}, f32[2,4,160,1]{2,1,3,0:T(4,128)S(1)}, u32[]{:S(2)}) copy-start(f32[2,4,160,1]{2,1,3,0:T(4,128)S(1)} %get-tuple-element.460) | copy-start | bytes 15364
  107.2 43.5 %copy-start.8 = (bf16[2,160,4,64]{1,3,2,0:T(8,128)(2,1)}, bf16[2,160,4,64]{1,3,2,0:T(8,128)(2,1)S(1)}, u32[]{:S(2)}) copy-start(bf16[2,160,4,64]{1,3,2,0:T(8,128)(2,1)S(1)} %get-tuple-element.537) | copy-start | bytes 491524
  107.2 40.0 %copy-start.13 = (bf16[2,160,512]{2,1,0:T(8,128)(2,1)S(1)}, bf16[2,160,512]{2,1,0:T(8,128)(2,1)}, u32[]{:S(2)}) copy-start(bf16[2,160,512]{2,1,0:T(8,128)(2,1)} %param.30) | copy-start | bytes 983044
  108.6 42.2 %copy-start.88 = (f32[512]{0:T(512)S(1)}, f32[512]{0:T(512)}, u32[]{:S(2)}) copy-start(f32[512]{0:T(512)} %param.39) | copy-start | bytes 6148
  108.6 42.2 %copy-start.93 = (f32[512]{0:T(512)S(1)}, f32[512]{0:T(512)}, u32[]{:S(2)}) copy-start(f32[512]{0:T(512)} %param.40) | copy-start | bytes 6148
  108.7 42.2 %copy-start.17 = (bf16[320,256]{0,1:T(8,128)(2,1)}, bf16[320,256]{0,1:T(8,128)(2,1)S(1)}, u32[]{:S(2)}) copy-start(bf16[320,256]{0,1:T(8,128)(2,1)S(1)} %reshape.344) | copy-start | bytes 491524
  110.7 40.5 %copy-start.57 = (bf16[4,512,16]{1,2,0:T(8,128)(2,1)S(1)}, bf16[4,512,16]{1,2,0:T(8,128)(2,1)}, u32[]{:S(2)}) copy-start(bf16[4,512,16]{1,2,0:T(8,128)(2,1)} %param.50) | copy-start | bytes 196612
  110.7 40.8 %copy-start.71 = (bf16[4,16,16]{2,1,0:T(8,128)(2,1)S(1)}, bf16[4,16,16]{2,1,0:T(8,128)(2,1)}, u32[]{:S(2)}) copy-start(bf16[4,16,16]{2,1,0:T(8,128)(2,1)} %param.51) | copy-start | bytes 6148
  111.4 44.6 %all-to-all-start.1 = ((bf16[2,4,4]{2,0,1:T(2,128)(2,1)}), bf16[2,4,4]{2,0,1:T(2,128)(2,1)S(1)}, u32[]{:S(2)}, u32[]{:S(2)}) async-start(bf16[2,4,4]{2,0,1:T(2,128)(2,1)} %broadcast_in_dim.130), calls=%async_computation.1 | async-start | bytes 4096 | tf_op jit(solution)/shard_map/all_to_all | solution.py:356
  118.0 31.2 %copy-start.82 = (f32[320]{0:T(512)}, f32[320]{0:T(512)S(1)}, u32[]{:S(2)}) copy-start(f32[320]{0:T(512)S(1)} %div.61) | copy-start | bytes 3844
  118.1 31.1 %copy-start.84 = (f32[320]{0:T(512)}, f32[320]{0:T(512)S(1)}, u32[]{:S(2)}) copy-start(f32[320]{0:T(512)S(1)} %rsqrt.22) | copy-start | bytes 3844
  118.2 35.8 %copy-start.79 = (s32[320,2]{0,1:T(2,128)}, s32[320,2]{0,1:T(2,128)S(1)}, u32[]{:S(2)}) copy-start(s32[320,2]{0,1:T(2,128)S(1)} %eq.60) | copy-start | bytes 7684
  123.3 28.1 %copy-start.67 = (bf16[512,16]{0,1:T(8,128)(2,1)}, bf16[512,16]{0,1:T(8,128)(2,1)S(1)}, u32[]{:S(2)}) copy-start(bf16[512,16]{0,1:T(8,128)(2,1)S(1)} %all_gather.23) | copy-start | bytes 49156
  123.3 37.7 %copy-start.87 = (s32[2,160,2]{1,2,0:T(2,128)}, s32[2,160,2]{1,2,0:T(2,128)S(1)}, u32[]{:S(2)}) copy-start(s32[2,160,2]{1,2,0:T(2,128)S(1)} %compare_select_fusion) | copy-start | bytes 7684
  151.0 10.8 %copy-start.11 = (bf16[320,512]{1,0:T(8,128)(2,1)}, bf16[320,512]{1,0:T(8,128)(2,1)S(1)}, u32[]{:S(2)}) copy-start(bf16[320,512]{1,0:T(8,128)(2,1)S(1)} %add_convert_fusion.2) | copy-start | bytes 983044
  151.4 10.4 %copy-start.49 = (bf16[320,64]{0,1:T(8,128)(2,1)}, bf16[320,64]{0,1:T(8,128)(2,1)S(1)}, u32[]{:S(2)}) copy-start(bf16[320,64]{0,1:T(8,128)(2,1)S(1)} %fusion.90) | copy-start | bytes 122884
  151.7 10.1 %copy-start.77 = (f32[320]{0:T(512)}, f32[320]{0:T(512)S(1)}, u32[]{:S(2)}) copy-start(f32[320]{0:T(512)S(1)} %fusion.115) | copy-start | bytes 3844
  151.9 10.0 %copy-start.92 = (f32[2,160,2]{1,2,0:T(2,128)}, f32[2,160,2]{1,2,0:T(2,128)S(1)}, u32[]{:S(2)}) copy-start(f32[2,160,2]{1,2,0:T(2,128)S(1)} %copy.192) | copy-start | bytes 7684
  156.0 18.0 %all-to-all-start.3 = ((bf16[2,16,30,512]{3,0,2,1:T(2,128)(2,1)}), bf16[2,16,30,512]{3,0,2,1:T(2,128)(2,1)}, u32[]{:S(2)}, u32[]{:S(2)}) async-start(bf16[2,16,30,512]{3,0,2,1:T(2,128)(2,1)} %bitcast.448), calls=%async_computation.3 | async-start | bytes 1966080 | tf_op jit(solution)/shard_map/all_to_all | solution.py:381
  161.3 21.6 %copy-start.20 = (bf16[2,160,480]{2,1,0:T(8,128)(2,1)}, bf16[2,160,480]{2,1,0:T(8,128)(2,1)S(1)}, u32[]{:S(2)}) copy-start(bf16[2,160,480]{2,1,0:T(8,128)(2,1)S(1)} %convert_reduce_fusion) | copy-start | bytes 921604
  174.0 18.1 %all-to-all-start = ((bf16[2,16,30,512]{3,0,2,1:T(2,128)(2,1)}), bf16[2,16,30,512]{3,0,2,1:T(2,128)(2,1)}, u32[]{:S(2)}, u32[]{:S(2)}) async-start(bf16[2,16,30,512]{3,0,2,1:T(2,128)(2,1)} %bitcast.447), calls=%async_computation | async-start | bytes 1966080 | tf_op jit(solution)/shard_map/all_to_all | solution.py:355
  179.1 115.5 %all-reduce.14.cloned.1.call-start = ((), (), s32[]{:S(2)}) async-start(), calls=%async_computation.12 | async-start | bytes 5242880 | tf_op jit(solution)/shard_map/psum | solution.py:161
  198.0 16.4 %copy-start.32 = (bf16[8,4,30,64]{3,2,0,1:T(8,128)(2,1)}, bf16[8,4,30,64]{3,2,0,1:T(8,128)(2,1)S(1)}, u32[]{:S(2)}) copy-start(bf16[8,4,30,64]{3,2,0,1:T(8,128)(2,1)S(1)} %fusion.84) | copy-start | bytes 368644
  298.1 18.1 %all-to-all-start.2 = ((bf16[8,4,30,512]{3,1,2,0:T(4,128)(2,1)}), bf16[8,4,30,512]{3,1,2,0:T(4,128)(2,1)}, u32[]{:S(2)}, u32[]{:S(2)}) async-start(bf16[8,4,30,512]{3,1,2,0:T(4,128)(2,1)} %copy.200), calls=%async_computation.2 | async-start | bytes 1966080 | tf_op jit(solution)/shard_map/all_to_all | solution.py:359
  316.2 18.1 %all-to-all-start.4 = ((bf16[8,4,30,512]{3,1,2,0:T(4,128)(2,1)}), bf16[8,4,30,512]{3,1,2,0:T(4,128)(2,1)}, u32[]{:S(2)}, u32[]{:S(2)}) async-start(bf16[8,4,30,512]{3,1,2,0:T(4,128)(2,1)} %copy.205), calls=%async_computation.4 | async-start | bytes 1966080 | tf_op jit(solution)/shard_map/all_to_all | solution.py:385
  321.3 65.9 %reduce-scatter.9.cloned.1.call-start = ((), (), s32[]{:S(2)}) async-start(), calls=%async_computation.9 | async-start | bytes 819200
  334.3 8.0 copy-start.30
  334.3 8.0 copy-start.43
  336.4 7.6 copy-start.62
  337.7 7.1 copy-start.24
  357.6 7.0 copy-start.35
  364.3 42.7 %reduce-scatter.7.cloned.1.call-start = ((), (), s32[]{:S(2)}) async-start(), calls=%async_computation.8 | async-start | bytes 819200
  378.9 85.7 %all-reduce.8.cloned.1.call-start = ((), (), s32[]{:S(2)}) async-start(), calls=%async_computation.7 | async-start | bytes 655360 | tf_op jit(solution)/shard_map/psum | solution.py:437
  379.0 7.3 copy-start.7
  379.0 7.3 copy-start.48
  381.5 26.9 %copy-start.61 = (bf16[2,160,4,64]{1,3,2,0:T(8,128)(2,1)S(1)}, bf16[2,160,4,64]{1,3,2,0:T(8,128)(2,1)}, u32[]{:S(2)}) copy-start(bf16[2,160,4,64]{1,3,2,0:T(8,128)(2,1)} %get-tuple-element.118) | copy-start | bytes 491524
  385.5 26.7 %copy-start.44 = (f32[4,512,16]{1,2,0:T(8,128)}, f32[4,512,16]{1,2,0:T(8,128)S(1)}, u32[]{:S(2)}) copy-start(f32[4,512,16]{1,2,0:T(8,128)S(1)} %fusion.92) | copy-start | bytes 393220
  388.6 23.7 %copy-start.46 = (bf16[320,64]{0,1:T(8,128)(2,1)S(1)}, bf16[320,64]{0,1:T(8,128)(2,1)}, u32[]{:S(2)}) copy-start(bf16[320,64]{0,1:T(8,128)(2,1)} %copy-done.45) | copy-start | bytes 122884
  408.4 11.0 %copy-start.70 = (f32[320,4]{0,1:T(4,128)S(1)}, f32[320,4]{0,1:T(4,128)}, u32[]{:S(2)}) copy-start(f32[320,4]{0,1:T(4,128)} %copy-done.69) | copy-start | bytes 15364
  408.4 11.0 %copy-start.15 = (f32[320,512]{1,0:T(8,128)S(1)}, f32[320,512]{1,0:T(8,128)}, u32[]{:S(2)}) copy-start(f32[320,512]{1,0:T(8,128)} %get-tuple-element.282) | copy-start | bytes 1966084
  408.4 11.0 %copy-start.81 = (f32[512]{0:T(512)S(1)}, f32[512]{0:T(512)}, u32[]{:S(2)}) copy-start(f32[512]{0:T(512)} %param.37) | copy-start | bytes 6148
  408.4 11.0 %copy-start.89 = (f32[512]{0:T(512)S(1)}, f32[512]{0:T(512)}, u32[]{:S(2)}) copy-start(f32[512]{0:T(512)} %param.38) | copy-start | bytes 6148
  412.2 401.0 %all-reduce.10.cloned.1.call-start = ((), (), s32[]{:S(2)}) async-start(), calls=%async_computation.10 | async-start | bytes 43778048 | tf_op jit(solution)/shard_map/psum | solution.py:461
  412.6 7.7 copy-start.28
  420.3 44.3 %copy-start.64 = (bf16[4,512,16]{1,2,0:T(8,128)(2,1)S(1)}, bf16[4,512,16]{1,2,0:T(8,128)(2,1)}, u32[]{:S(2)}) copy-start(bf16[4,512,16]{1,2,0:T(8,128)(2,1)} %param.46) | copy-start | bytes 196612
  420.3 45.8 %copy-start.14 = (bf16[2,160,512]{2,1,0:T(8,128)(2,1)S(1)}, bf16[2,160,512]{2,1,0:T(8,128)(2,1)}, u32[]{:S(2)}) copy-start(bf16[2,160,512]{2,1,0:T(8,128)(2,1)} %param.30) | copy-start | bytes 983044
  420.3 45.8 %copy-start.83 = (f32[320]{0:T(512)S(1)}, f32[320]{0:T(512)}, u32[]{:S(2)}) copy-start(f32[320]{0:T(512)} %copy-done.82) | copy-start | bytes 3844
  420.3 45.8 %copy-start.85 = (f32[320]{0:T(512)S(1)}, f32[320]{0:T(512)}, u32[]{:S(2)}) copy-start(f32[320]{0:T(512)} %copy-done.84) | copy-start | bytes 3844
  821.3 11.4 %slice-start = ((s8[8388608]{0:T(1024)(128)(4,1)}), s8[4194304]{0:T(1024)(128)(4,1)S(1)}, s32[]{:S(2)}) async-start(s8[8388608]{0:T(1024)(128)(4,1)} %bitcast.437), calls=%async_computation.13 | async-start | bytes 8388608
  824.6 8.0 slice-start.1
  (51 other events, 159.2 us)
Sparse Core Ops, SparseCore 0:
  110.8 35.3 all-reduce.11
  220.4 74.1 all-reduce.13
  364.4 19.1 reduce-scatter.8
  385.9 21.0 reduce-scatter.6
  412.3 25.6 all-reduce.7
  445.5 367.6 all-reduce.9
where the time goes:
time: 857 us; the launch traced here: 845 us
  waiting for transfers between devices  490 us (57%)
  blocking collectives  131 us (15%)
  local copies, waits for them, and re-layouts  93.5 us (11%)
  matrix products  70.4 us (8%)
  starting transfers between devices  27.3 us (3%)
  other arithmetic  16.8 us (2%)
  between operations  16.1 us (2%)
    psum x1, waiting for transfers between devices, per_device(): lax.psum((full_attend_down, full_attend_up, full_mixing_down, full_mixing...  346 us
    psum x1, waiting for transfers between devices, expert_forward(): lax.psum(partial_out.astype(jnp.bfloat16), 'tp').astype(jnp.float32)  74.3 us
    psum x1, blocking collectives, per_device(): lax.psum((full_attend_down, full_attend_up, full_mixing_down, full_mixing...  43.3 us
    unnamed x201, local copies, waits for them, and re-layouts  41.6 us
    all_gather x1, blocking collectives, per_device(): lax.all_gather(value_block, 'ctx', axis=1, tiled=True)  24.5 us
    all_gather x1, blocking collectives, per_device(): lax.all_gather(key_block, 'ctx', axis=1, tiled=True)  22.8 us
    psum x1, waiting for transfers between devices, per_device(): summed_mix, summed_lift = lax.psum((partial_mix, partial_lift), 'tp')  21.9 us
    unnamed x8, waiting for transfers between devices  18.5 us
  transfers between devices with their start and end apart: 11, of which 8 were waited for; matrix products, arithmetic and copies ran while one was open for 7% of the time, Pallas kernels for 0%

commit v1 on v0

v1 whole, which is shorter than its diff:
```python
import functools
import types

import jax
import jax.numpy as jnp
from jax import lax
from jax.experimental import pallas as pl
from jax.experimental.pallas import tpu as pltpu
from jax.sharding import PartitionSpec as P

D = 512
HEADS = 8
HD = 64
FF = 2048
EXPERTS = 16
TOP = 2
RANK = 16
SETS = 4
CAP = 30
SLOTS = 32
WIDTH = SETS * RANK
LIVE_ROW = 2 * TOP
SET_ROW = LIVE_ROW + 1
CRITICAL = D + 128
EXPERT_ROWS = 256

EPSILON = 1e-06
MASKED = -1e30
SQRT_HALF = 0.7071067811865476
INV_ROOT_TWO_PI = 0.3989422804014327
F32 = jnp.float32
BF16 = jnp.bfloat16
MESH = pl.DeviceIdType.MESH
ANY = pl.BlockSpec(memory_space=pl.ANY)
IN_SMEM = pl.BlockSpec(memory_space=pltpu.SMEM)
IN_VMEM = pl.BlockSpec(memory_space=pltpu.VMEM)


def matmul(left_side, right_side):
    return jnp.dot(left_side, right_side, preferred_element_type=F32)


def inner_rows(left_side, right_side):
    return lax.dot_general(
        left_side, right_side, (((0,), (0,)), ((), ())), preferred_element_type=F32
    )


def times_transposed(left_side, right_side):
    return lax.dot_general(
        left_side, right_side, (((1,), (1,)), ((), ())), preferred_element_type=F32
    )


def normalize(values, gain_row, shift_row):
    centred = values - jnp.mean(values, axis=-1, keepdims=True)
    spread = jnp.mean(centred * centred, axis=-1, keepdims=True)
    factor = lax.rsqrt(spread + EPSILON)
    normed = centred * factor
    return (normed * gain_row + shift_row, normed, factor)


def normalize_back(grad_out, normed, factor, gain_row):
    scaled = grad_out * gain_row
    return factor * (
        scaled
        - jnp.mean(scaled, axis=-1, keepdims=True)
        - normed * jnp.mean(scaled * normed, axis=-1, keepdims=True)
    )


def add_rounded(*parts):
    total = parts[0].astype(F32)
    for part in parts[1:]:
        total = total + part.astype(F32)
    return total.astype(BF16)


def split_sum(values, ones):
    high = values.astype(BF16)
    low = (values - high.astype(F32)).astype(BF16)
    return matmul(high, ones) + matmul(low, ones)


def put_lanes(columns, width):
    lane = lax.broadcasted_iota(jnp.int32, (columns[0].shape[0], width), 1)
    total = jnp.zeros((columns[0].shape[0], width), F32)
    for k, column in enumerate(columns):
        total = jnp.where(lane == k, column, total)
    return total


def half_masks():
    lane = lax.broadcasted_iota(jnp.int32, (1, 2 * HD), 1)
    even = (lane < HD).astype(F32)
    return even, 1.0 - even


def stack_pair(rows, masks, factor=1.0):
    wide = rows.astype(F32) * factor
    return jnp.concatenate([wide * masks[0], wide * masks[1]], axis=0).astype(BF16)


def join_pair(rows, masks):
    half = rows.shape[0] // 2
    return rows[:half] * masks[0] + rows[half:] * masks[1]


def small_rows(tiles, plane):
    return -(-tiles * WIDTH // (plane * 16)) * 16


class Wire:
    def __init__(self, send, recv, local):
        self.send, self.recv, self.local = send, recv, local
        self.used = self.used_local = 0

    def copy(self, src, dst, device):
        k = self.used
        self.used += 1
        assert k < self.send.shape[0]
        return pltpu.make_async_remote_copy(
            src_ref=src,
            dst_ref=dst,
            send_sem=self.send.at[k],
            recv_sem=self.recv.at[k],
            device_id=device,
            device_id_type=MESH,
        )

    def near(self, src, dst):
        k = self.used_local
        self.used_local += 1
        assert k < self.local.shape[0]
        return pltpu.make_async_copy(src, dst, self.local.at[k])


class Place:
    def __init__(self, sizes):
        self.dp_size, self.ctx_size, self.tp_size = sizes
        self.chips = self.dp_size // 2
        self.plane = self.dp_size * self.tp_size
        self.dp = lax.axis_index("dp")
        self.ctx = lax.axis_index("ctx")
        self.tp = lax.axis_index("tp")
        self.chip = lax.div(self.dp, 2)
        self.core = lax.rem(self.dp, 2)
        self.sibling = self.chip * 2 + (1 - self.core)
        self.other_tp = lax.rem(self.tp + 1, 2)
        self.me = self.dp * self.tp_size + self.tp
        self.is_mid = jnp.logical_and(self.ctx >= 1, self.ctx <= 2)
        self.is_end = jnp.logical_not(self.is_mid)
        self.inner = lax.div(self.ctx, 2)
        self.partner = jnp.where(self.is_mid, self.inner * 3, 1 + self.inner)
        self.other_mid = 2 - self.inner
        self.peers = []
        for k in range(1, self.plane):
            peer = lax.rem(self.me + k, self.plane)
            self.peers.append((lax.div(peer, self.tp_size), lax.rem(peer, self.tp_size)))

    def ahead(self, i, j):
        return (
            lax.rem(self.chip + i, self.chips) * 2 + self.core,
            lax.rem(self.tp + j, self.tp_size),
        )

    def behind(self, i, j):
        return self.ahead(self.chips - i, self.tp_size - j)

    def offsets(self, over_tp=True):
        return [
            (i, j)
            for i in range(self.chips)
            for j in range(self.tp_size if over_tp else 1)
            if i or j
        ]

    def greet(self):
        barrier = pltpu.get_barrier_semaphore()
        for dp, tp in self.peers:
            pl.semaphore_signal(
                barrier, inc=1, device_id={"dp": dp, "tp": tp}, device_id_type=MESH
            )
        pl.semaphore_signal(
            barrier, inc=1, device_id={"ctx": self.partner}, device_id_type=MESH
        )

        @pl.when(self.is_mid)
        def _():
            pl.semaphore_signal(
                barrier, inc=1, device_id={"ctx": self.other_mid}, device_id_type=MESH
            )

        pl.semaphore_wait(barrier, self.plane + jnp.where(self.is_mid, 1, 0))


class Spread:
    def __init__(self, place, wire, source, slot, over_tp=True, direct=False, near=True):
        self.place, self.wire, self.source, self.slot = place, wire, source, slot
        self.over_tp = over_tp
        self.relay = over_tp and not direct and place.chips == 2 and place.tp_size == 2
        self.near = near
        self.flights, self.across, self.beside, self.here = [], None, [], None

    def to_sibling(self, source, spot):
        copy = self.wire.copy(source, spot, {"dp": self.place.sibling})
        copy.start()
        self.beside.append(copy)

    def start(self):
        place = self.place
        spot = self.slot(place.dp, place.tp)
        for i, j in place.offsets(self.over_tp):
            if self.relay and i and j:
                continue
            dp, tp = place.ahead(i, j)
            copy = self.wire.copy(self.source, spot, {"dp": dp, "tp": tp})
            copy.start()
            self.flights.append((copy, i, j))
        self.to_sibling(self.source, spot)
        if self.near:
            self.here = self.wire.near(self.source, spot)
            self.here.start()

    def forward(self):
        for copy, i, j in sorted(self.flights, key=lambda f: f[1]):
            copy.wait_recv()
            got = self.slot(*self.place.behind(i, j))
            if self.relay and j:
                dp, tp = self.place.ahead(1, 0)
                self.across = self.wire.copy(got, got, {"dp": dp, "tp": tp})
                self.across.start()
            self.to_sibling(got, got)

    def diagonal(self):
        if self.relay:
            self.across.wait_recv()
            got = self.slot(*self.place.behind(1, 1))
            self.to_sibling(got, got)

    def finish(self):
        for copy in self.beside:
            copy.wait_recv()
        if self.near:
            self.here.wait()

    def drain(self):
        for copy, _, _ in self.flights:
            copy.wait_send()
        if self.relay:
            self.across.wait_send()
        for copy in self.beside:
            copy.wait_send()

    @staticmethod
    def remote(sizes, over_tp=True):
        return 2 * (sizes[0] // 2 * (sizes[2] if over_tp else 1) - 1) + 1


class Chain:
    def __init__(self, place, wire, sources, slots, over, with_own):
        self.place, n = place, place.ctx_size
        self.steps = n - 1
        to_tp = {"tp": place.other_tp}
        self.right, self.left, self.over_right, self.over_left = {}, {}, {}, {}
        self.own, self.here = [], []
        for source, slot in zip(sources, slots):
            spot = slot(place.ctx, place.tp)
            if with_own:
                self.own.append(wire.copy(source, spot, to_tp))
                self.here.append(wire.near(source, spot))
        for s in range(1, n):
            back = [slot(jnp.maximum(place.ctx - (s - 1), 0), place.tp) for slot in slots]
            ahead = [slot(jnp.minimum(place.ctx + (s - 1), n - 1), place.tp) for slot in slots]
            got_right = [slot(jnp.maximum(place.ctx - s, 0), place.tp) for slot in slots]
            got_left = [slot(jnp.minimum(place.ctx + s, n - 1), place.tp) for slot in slots]
            to_right = {"ctx": jnp.minimum(place.ctx + 1, n - 1)}
            to_left = {"ctx": jnp.maximum(place.ctx - 1, 0)}
            self.right[s] = [
                wire.copy(a if s == 1 else b, b, to_right) for a, b in zip(sources, back)
            ]
            self.left[s] = [
                wire.copy(a if s == 1 else b, b, to_left) for a, b in zip(sources, ahead)
            ]
            self.over_right[s] = [wire.copy(b, b, to_tp) for b, o in zip(got_right, over) if o]
            self.over_left[s] = [wire.copy(b, b, to_tp) for b, o in zip(got_left, over) if o]

    def sends_right(self, s):
        return jnp.logical_and(self.place.ctx >= s - 1, self.place.ctx < self.steps)

    def sends_left(self, s):
        return jnp.logical_and(self.place.ctx <= self.steps + 1 - s, self.place.ctx > 0)

    def gets_right(self, s):
        return self.place.ctx >= s

    def gets_left(self, s):
        return self.place.ctx <= self.steps - s

    @staticmethod
    def all_of(copies, verb):
        for copy in copies:
            getattr(copy, verb)()

    def start(self):
        pl.when(self.sends_right(1))(lambda: self.all_of(self.right[1], "start"))
        pl.when(self.sends_left(1))(lambda: self.all_of(self.left[1], "start"))
        self.all_of(self.own + self.here, "start")

    def step(self, s):
        def passed(got, over, sends):
            def run():
                self.all_of(got[s], "wait_recv")
                if s < self.steps:
                    pl.when(sends(s + 1))(lambda: self.all_of(got[s + 1], "start"))
                self.all_of(over[s], "start")

            return run

        pl.when(self.gets_right(s))(passed(self.right, self.over_right, self.sends_right))
        pl.when(self.gets_left(s))(passed(self.left, self.over_left, self.sends_left))

    def landed(self, s):
        pl.when(self.gets_right(s))(lambda: self.all_of(self.over_right[s], "wait_recv"))
        pl.when(self.gets_left(s))(lambda: self.all_of(self.over_left[s], "wait_recv"))

    def finish_own(self):
        self.all_of(self.own, "wait_recv")
        self.all_of(self.here, "wait")

    def drain(self):
        self.all_of(self.own, "wait_send")
        for s in range(1, self.steps + 1):
            pl.when(self.gets_right(s))(lambda: self.all_of(self.over_right[s], "wait_send"))
            pl.when(self.gets_left(s))(lambda: self.all_of(self.over_left[s], "wait_send"))
            pl.when(self.sends_right(s))(lambda: self.all_of(self.right[s], "wait_send"))
            pl.when(self.sends_left(s))(lambda: self.all_of(self.left[s], "wait_send"))

    @staticmethod
    def remote(n, arrays):
        return arrays * (1 + 4 * (n - 1))


def layer_kernel(sizes, names, *refs):
    r = types.SimpleNamespace(**dict(zip(names, refs)))
    place = Place(sizes)
    wire = Wire(r.send, r.recv, r.local)
    plane = place.plane
    images, block = r.tokens.shape[:2]
    half = block // place.tp_size
    count = images * half
    seq = place.ctx_size * block
    experts, _, hidden_units = r.up_weight.shape
    all_images = place.dp_size * images
    owned = place.dp * experts
    start = pl.multiple_of(place.tp * half, 16)
    own_start = pl.multiple_of(place.ctx * block + place.tp * half, 16)
    own = pl.ds(own_start, half)
    masks = half_masks()
    scale = HD**-0.5

    pending = {}

    def load(name, source, target):
        pending[name] = wire.near(source, target)
        pending[name].start()

    def need(*wanted):
        for name in wanted:
            if name in pending:
                pending.pop(name).wait()

    whole = pl.ds(pl.multiple_of(place.ctx * block, 16), block)
    load("tokens", r.tokens, r.tokens_all.at[:, whole, :])
    for name in (
        "attend_low", "attend_high", "mixing_low", "mixing_high", "router_low", "router_high",
    ):
        load(name, getattr(r, name), getattr(r, "v_" + name))
    wide = pl.ds(pl.multiple_of(place.tp * hidden_units, 128), hidden_units)
    for e in range(experts):
        load(("a_first", e), r.first_a.at[:, owned + e], r.v_first_a.at[e])
        load(("b_first", e), r.first_b.at[:, owned + e, :, wide], r.v_first_b.at[e])
        load(("up", e), r.up_weight.at[e], r.v_up.at[e])
        load(("a_second", e), r.second_a.at[:, owned + e, :, wide], r.v_second_a.at[e])
        load(("b_second", e), r.second_b.at[:, owned + e], r.v_second_b.at[e])
        load(("down", e), r.down_weight.at[e], r.v_down.at[e])
    r.ints[:, 0:TOP, :] = r.routes_t[...]
    r.ints[:, TOP : 2 * TOP, :] = r.slots_t[...]
    lane_set = lax.div(lax.broadcasted_iota(jnp.int32, (1, WIDTH), 1), RANK)
    picks = []
    for i in range(images):
        r.ints[i, LIVE_ROW : LIVE_ROW + 1, :] = r.token_mask[i : i + 1, :] * r.image_mask[i]
        r.ints[i, SET_ROW:, :] = jnp.full((8 - SET_ROW, block), r.adapter_set[i], jnp.int32)
        picks.append((lane_set == r.adapter_set[i]).astype(F32))
    gain_one, shift_one = r.gains[0:1, :], r.gains[1:2, :]
    gain_two, shift_two = r.gains[2:3, :], r.gains[3:4, :]

    place.greet()

    rows, lanes = r.mixing.shape

    def at_rows(dp):
        return pl.ds(pl.multiple_of(dp * rows, 16), rows)

    def at_lanes(tp):
        return pl.ds(pl.multiple_of(tp * lanes, 128), lanes)

    def token_slot(ctx, tp):
        at = pl.multiple_of(ctx * block + tp * half, 16)
        return r.tokens_all.at[:, pl.ds(at, half), :]

    tokens_chain = Chain(
        place, wire, [r.tokens.at[:, pl.ds(start, half), :], r.ints],
        [token_slot, lambda ctx, tp: r.ctx_ints.at[ctx]], [True, False], False,
    )
    weights = Spread(
        place, wire, r.weights, lambda dp, tp: r.weights_all.at[:, at_rows(dp), at_lanes(tp)]
    )
    mixing = Spread(
        place, wire, r.mixing, lambda dp, tp: r.mixing_all.at[at_rows(dp), at_lanes(tp)]
    )
    numbers = Spread(
        place, wire, r.ints, lambda dp, tp: r.ints_all.at[pl.ds(dp * 2, 2)], over_tp=False
    )
    router = Spread(place, wire, r.router, lambda dp, tp: r.router_all.at[dp], over_tp=False)
    cotangents = Spread(
        place, wire, r.cotangent, lambda dp, tp: r.cot_all.at[pl.ds(dp * 2, 2)], over_tp=False
    )
    r.ctx_ints[place.ctx] = r.ints[...]
    tokens_chain.start()
    weights.start()
    numbers.start()
    router.start()
    mixing.start()
    cotangents.start()
    weights.forward()
    tokens_chain.step(1)
    weights.diagonal()
    tokens_chain.step(2)
    numbers.forward()
    router.forward()
    weights.finish()
    need("tokens", "attend_low", "attend_high")

    block_picks = jnp.concatenate(
        [jnp.broadcast_to(pick, (block, WIDTH)) for pick in picks], axis=0
    )
    own_sets = jnp.concatenate(
        [jnp.broadcast_to(pick, (half, WIDTH)) for pick in picks], axis=0
    )
    attend_low = r.v_attend_low[...].reshape(WIDTH, D)

    def high(p):
        return r.v_attend_high[:, p].reshape(WIDTH, D)

    def project(k, _):
        ctx = place.ctx
        first = jnp.where(ctx == 3, 2, ctx + 1)
        second = jnp.where(ctx == 0, 2, jnp.where(ctx == 1, 0, 1))
        third = jnp.where(ctx < 2, 3, 0)
        which = jnp.where(
            k == 0, ctx, jnp.where(k == 1, first, jnp.where(k == 2, second, third))
        )
        at = pl.ds(pl.multiple_of(which * block, 16), block)
        values = jnp.concatenate([r.tokens_all[i, at, :] for i in range(images)], axis=0)
        normed = normalize(values.astype(F32), gain_one, shift_one)[0].astype(BF16)
        lift = (times_transposed(normed, attend_low) * block_picks).astype(BF16)
        for i in range(images):
            r.lift_all[i, at, :] = lift[i * block : (i + 1) * block]
        for p in range(3):
            made = (matmul(normed, r.weights_all[p]) + matmul(lift, high(p))).astype(BF16)
            for i in range(images):
                r.joined[p, i, at, :] = made[i * block : (i + 1) * block]
        return 0

    def project_blocks(low, up):
        lax.fori_loop(low, up, project, 0)

    project_blocks(0, 1)
    tokens_chain.step(3)
    tokens_chain.landed(1)
    mixing.forward()
    project_blocks(1, 2)
    tokens_chain.landed(2)
    project_blocks(2, 3)
    cotangents.forward()
    mixing.diagonal()
    tokens_chain.landed(3)
    project_blocks(3, 4)
    mixing.finish()
    need("mixing_low", "mixing_high")
    mixing_low = r.v_mixing_low[...].reshape(WIDTH, D)
    mixing_high = r.v_mixing_high[...].reshape(WIDTH, D)

    def open_keys(i):
        return (
            jnp.concatenate(
                [
                    r.ctx_ints[n, i, LIVE_ROW : LIVE_ROW + 1, :]
                    for n in range(place.ctx_size)
                ],
                axis=1,
            )
            > 0
        )

    for i in range(images):
        r.keys_open[i : i + 1, :] = open_keys(i).astype(F32)
        token_rows = r.tokens_all[i, own, :].astype(F32)
        r.own_in[i] = normalize(token_rows, gain_one, shift_one)[0].astype(BF16)
        keys_open = r.keys_open[i : i + 1, :] > 0
        part = slice(i * half, (i + 1) * half)
        logs = []
        for j in range(HEADS // 2):
            at = slice(j * 2 * HD, (j + 1) * 2 * HD)
            q = stack_pair(r.joined[0, i, own, at], masks, scale)
            scores = times_transposed(q, r.joined[1, i, :, at])
            scores = jnp.where(keys_open, scores, MASKED)
            top = jnp.max(scores, axis=-1, keepdims=True)
            powers = jnp.exp(scores - top)
            total = jnp.sum(powers, axis=-1, keepdims=True)
            weights_att = (powers * (1.0 / total)).astype(BF16)
            mixed = join_pair(matmul(weights_att, r.joined[2, i, :, at]), masks)
            r.head_mix[part, at] = mixed.astype(BF16)
            log = jnp.maximum(top + jnp.log(total), -1e29)
            logs += [log[:half], log[half:]]
        r.logs[part, :] = put_lanes(logs, 128)
        mix = r.head_mix[part, :]
        lift = (times_transposed(mix, mixing_low) * picks[i]).astype(BF16)
        r.mixing_lift[part, :] = lift
        hidden = token_rows + times_transposed(mix, r.mixing_all[...]) + matmul(lift, mixing_high)
        r.hidden[part, :] = hidden
        r.expert_in[i] = normalize(hidden, gain_two, shift_two)[0].astype(BF16)

    def rows_slot(dp, tp):
        at = pl.multiple_of(tp * half, 16)
        return r.rows_all.at[pl.ds(dp * 2, 2), pl.ds(at, half), :]

    expert_rows = Spread(place, wire, r.expert_in, rows_slot, direct=True)
    expert_rows.start()

    slots = experts * SLOTS
    cotangents.finish()
    numbers.finish()
    router.finish()
    need("router_low", "router_high")
    router_low = r.v_router_low[...].reshape(WIDTH, D)
    router_high = r.v_router_high[...].reshape(WIDTH, EXPERTS)
    r.router_t[...] = jnp.concatenate([r.router_all[n] for n in range(place.dp_size)], axis=1)

    def targets(given, k):
        route, slot = given[k : k + 1, :], given[TOP + k : TOP + k + 1, :]
        local = route - owned
        here = (local >= 0) & (local < experts) & (slot < CAP)
        return jnp.where(here, local * SLOTS + slot, -1)

    def fill_slots(i, target, values):
        at = pl.ds(pl.multiple_of(i * SLOTS, SLOTS), SLOTS)
        for n in range(experts):
            target[n, at, :] = values[n * SLOTS : (n + 1) * SLOTS]

    def make_table(i, _):
        given = r.ints_all[i]
        slot = lax.broadcasted_iota(jnp.int32, (slots, block), 0)
        hot = jnp.zeros((slots, block), F32)
        for k in range(TOP):
            hot = jnp.where(slot == targets(given, k), 1.0, hot)
        hot = hot.astype(BF16)
        r.table[i] = hot
        fill_slots(i, r.grad_slots, matmul(hot, r.cot_all[i]).astype(BF16))
        return 0

    lax.fori_loop(0, all_images, make_table, 0)
    expert_rows.forward()
    expert_rows.finish()

    def dispatch(i, _):
        values = r.rows_all[i]
        given = r.ints_all[i]
        set_column = lax.div(lax.broadcasted_iota(jnp.int32, (WIDTH, 1), 0), RANK)
        pick = (set_column == given[SET_ROW : SET_ROW + 1, 0:1]).astype(F32)
        lift = (times_transposed(router_low, values) * pick).astype(BF16)
        logits = times_transposed(r.router_t[...], values) + inner_rows(router_high, lift)
        powers = jnp.exp(logits - jnp.max(logits, axis=0, keepdims=True))
        probs = powers / jnp.sum(powers, axis=0, keepdims=True)
        expert = lax.broadcasted_iota(jnp.int32, (EXPERTS, block), 0)
        slot = lax.broadcasted_iota(jnp.int32, (slots, block), 0)
        gated = jnp.zeros((slots, block), F32)
        for k in range(TOP):
            gate = jnp.sum(
                jnp.where(expert == given[k : k + 1, :], probs, 0.0), axis=0, keepdims=True
            )
            gated = jnp.where(slot == targets(given, k), gate, gated)
        column = jnp.broadcast_to(jnp.sum(gated, axis=1, keepdims=True), (slots, 128))
        fill_slots(i, r.gates, column)
        fill_slots(i, r.rows_in, matmul(r.table[i], values).astype(BF16))
        lane = lax.div(lax.broadcasted_iota(jnp.int32, (SLOTS, WIDTH), 1), RANK)
        at = pl.ds(pl.multiple_of(i * SLOTS, SLOTS), SLOTS)
        r.slot_sets[at, :] = (lane == given[SET_ROW : SET_ROW + 1, 0:1]).astype(F32)
        return 0

    lax.fori_loop(0, all_images, dispatch, 0)

    chunks = [
        (
            r.first.at[e], r.first_end.at[e], r.first_mid.at[e], r.first_stage.at[e],
            r.first_final.at[e],
            functools.partial(lambda e, dp, tp: r.first_all.at[dp, tp, e], e),
        )
        for e in range(experts)
    ]
    chunks += [
        (r.second_sum, r.second_end, r.second_mid, r.second_stage, r.second_final,
         lambda dp, tp: r.second_all.at[dp, tp]),
        (r.early_sum, r.early_end, r.early_mid, r.early_stage, r.early_final,
         lambda dp, tp: r.early_all.at[dp, tp]),
        (r.late_sum, r.late_end, r.late_mid, r.late_stage, r.late_final,
         lambda dp, tp: r.late_all.at[dp, tp]),
    ]
    inner, outer_half = place.inner, 1 - place.inner
    to_partner, to_mid = {"ctx": place.partner}, {"ctx": place.other_mid}
    flows, spreads = [], []
    for mine, end, mid, stage, final, slot in chunks:
        flows.append(
            dict(
                outer=wire.copy(mine.at[outer_half], end.at[outer_half], to_partner),
                inner=wire.copy(mine.at[inner], end.at[inner], to_partner),
                cross=wire.copy(stage, mid, to_mid),
                back=wire.copy(final.at[inner], final.at[inner], to_partner),
                share=wire.copy(final.at[inner], final.at[inner], to_mid),
                pass_on=wire.copy(final.at[outer_half], final.at[outer_half], to_partner),
            )
        )
        spreads.append(Spread(place, wire, final, slot))

    def send_end(k):
        @pl.when(place.is_end)
        def _():
            flows[k]["outer"].start()
            flows[k]["inner"].start()

    def mid_first(k):
        mine, end, mid, stage, final, slot = chunks[k]

        @pl.when(place.is_mid)
        def _():
            flows[k]["outer"].wait_recv()
            stage[...] = add_rounded(mine[outer_half], end[outer_half])
            flows[k]["cross"].start()

    def mid_second(k):
        mine, end, mid, stage, final, slot = chunks[k]

        @pl.when(place.is_mid)
        def _():
            flows[k]["inner"].wait_recv()
            flows[k]["cross"].wait_recv()
            final[inner] = add_rounded(mine[inner], end[inner], mid[...])
            flows[k]["share"].start()
            flows[k]["back"].start()

    def settle(k):
        @pl.when(place.is_mid)
        def _():
            flows[k]["share"].wait_recv()
            flows[k]["pass_on"].start()

        @pl.when(place.is_end)
        def _():
            flows[k]["back"].wait_recv()
            flows[k]["pass_on"].wait_recv()

        spreads[k].start()

    stages = (
        mid_first, mid_second, settle,
        lambda k: spreads[k].forward(), lambda k: spreads[k].diagonal(),
    )
    reached = [0] * len(chunks)
    SUM, FINAL, SENT, ONWARD, DONE = range(1, 6)
    second_at, early_at, late_at = experts, experts + 1, experts + 2

    def go(k, stage):
        while reached[k] < stage:
            stages[reached[k]](k)
            reached[k] += 1

    def go_first(*pairs):
        for k, stage in pairs:
            if k < experts:
                go(k, stage)

    def run_expert(e):
        need(("a_first", e), ("b_first", e), ("up", e))
        need(("a_second", e), ("b_second", e), ("down", e))
        a_first, b_first = r.v_first_a[e].reshape(WIDTH, D), r.v_first_b[e].reshape(WIDTH, -1)
        a_second = r.v_second_a[e].reshape(WIDTH, -1)
        b_second = r.v_second_b[e].reshape(WIDTH, D)
        sums = None
        size = min(EXPERT_ROWS, all_images * SLOTS)
        for c in range(all_images * SLOTS // size):
            at = slice(c * size, (c + 1) * size)
            rows = r.rows_in[e, at]
            grads = r.grad_slots[e, at].astype(F32)
            gate = r.gates[e, at][:, 0:1]
            sets = r.slot_sets[at]
            lifted = (times_transposed(rows, a_first) * sets).astype(BF16)
            before = matmul(rows, r.v_up[e]) + matmul(lifted, b_first)
            phi = 0.5 * (1.0 + lax.erf(before * SQRT_HALF))
            active = (before * phi).astype(BF16)
            slope = phi + before * (INV_ROOT_TWO_PI * jnp.exp(-0.5 * before * before))
            lowered = (times_transposed(active, a_second) * sets).astype(BF16)
            out = matmul(active, r.v_down[e]) + matmul(lowered, b_second)
            grad_out = (grads * gate).astype(BF16)
            grad_lowered = (times_transposed(grad_out, b_second) * sets).astype(BF16)
            grad_active = times_transposed(grad_out, r.v_down[e]) + matmul(grad_lowered, a_second)
            grad_before = (grad_active * slope).astype(BF16)
            grad_lifted = (times_transposed(grad_before, b_first) * sets).astype(BF16)
            grad_rows = times_transposed(grad_before, r.v_up[e]) + matmul(grad_lifted, a_first)
            made = [
                inner_rows(lifted, grad_before),
                inner_rows(grad_lowered, active),
                inner_rows(grad_lifted, rows),
                inner_rows(lowered, grad_out),
            ]
            sums = made if sums is None else [a + b for a, b in zip(sums, made)]
            lane = lax.broadcasted_iota(jnp.int32, (size, 128), 1)
            gate_grads = jnp.sum(out * grads, axis=1, keepdims=True)
            gate_grads = jnp.where(lane == owned + e, gate_grads, 0.0).astype(BF16)
            some = slice(c * size // SLOTS, (c + 1) * size // SLOTS)
            to = slice(e * SLOTS, (e + 1) * SLOTS)
            number = size // SLOTS
            r.payload[some, to, 0:D] = grad_rows.astype(BF16).reshape(number, SLOTS, D)
            r.payload[some, to, D:CRITICAL] = gate_grads.reshape(number, SLOTS, 128)
            r.payload[some, to, CRITICAL:] = (out * gate).astype(BF16).reshape(number, SLOTS, D)
        r.first[e, 0] = sums[0].astype(BF16)
        r.first[e, 1] = sums[1].astype(BF16)
        share = D // place.tp_size
        for number in range(2):
            for t in range(place.tp_size):
                r.second[t, number, e] = sums[2 + number][:, t * share : (t + 1) * share].astype(
                    BF16
                )

    for e in range(experts):
        run_expert(e)
        send_end(e)
        go_first(*((e - 1 - n, n + 1) for n in range(3) if e - 1 - n >= 0))

    second_swap = wire.copy(
        r.second.at[place.other_tp], r.second_got, {"tp": place.other_tp}
    )
    swap = wire.copy(r.partial.at[1 - place.core], r.from_sibling, {"dp": place.sibling})

    def combine(core):
        def run(chip, _):
            for n in range(images):
                i = (chip * 2 + core) * images + n
                made = inner_rows(r.table[i], r.payload[i]).astype(BF16)
                for t in range(place.tp_size):
                    r.partial[core, chip, t, n * half : (n + 1) * half, :] = made[
                        t * half : (t + 1) * half
                    ]
            return 0

        lax.fori_loop(0, place.chips, run, 0)

    combine(1 - place.core)
    swap.start()
    combine(place.core)
    swap.wait_recv()
    returns = []
    for at in (slice(0, CRITICAL), slice(CRITICAL, CRITICAL + D)):
        copies = []
        for i, j in place.offsets() + [(0, 0)]:
            dp, tp = place.ahead(i, j)
            chip = lax.div(dp, 2)
            index = i * place.tp_size + j
            both = add_rounded(
                r.partial[place.core, chip, tp, :, at], r.from_sibling[chip, tp, :, at]
            )
            if index:
                r.from_sibling[chip, tp, :, at] = both
                copy = wire.copy(
                    r.from_sibling.at[chip, tp, :, at],
                    r.received.at[index, :, at],
                    {"dp": dp, "tp": tp},
                )
                copy.start()
                copies.append(copy)
            else:
                r.received[0, :, at] = both
        returns.append(copies)
        if not at.start:
            second_swap.start()
    late_sends = [swap] + returns[0] + returns[1]
    last = experts - 1
    go_first((last - 2, SENT), (last - 1, FINAL), (last, SUM))
    go_first((last - 3, ONWARD))
    for copy in returns[0]:
        copy.wait_recv()

    def live_column(i):
        lane = lax.broadcasted_iota(jnp.int32, (half, block), 1)
        row = lax.broadcasted_iota(jnp.int32, (half, block), 0) + place.tp * half
        live = r.ints[i, LIVE_ROW : LIVE_ROW + 1, :].astype(F32)
        return jnp.sum(jnp.where(lane == row, live, 0.0), axis=1, keepdims=True)

    lives = [live_column(i) for i in range(images)]
    total = r.received[0, :, :CRITICAL].astype(F32)
    for k in range(1, r.received.shape[0]):
        total = total + r.received[k, :, :CRITICAL].astype(F32)
    hidden = r.hidden[...]
    grad_probs = total[:, D : D + EXPERTS]
    grad_output = jnp.concatenate(
        [
            r.cot_all[place.dp * images + i, pl.ds(start, half), :].astype(F32) * lives[i]
            for i in range(images)
        ],
        axis=0,
    )
    rows = r.expert_in[...].reshape(count, D)
    router_lift = (times_transposed(rows, router_low) * own_sets).astype(BF16)
    logits = times_transposed(rows, r.router_t[...]) + matmul(router_lift, router_high)
    powers = jnp.exp(logits - jnp.max(logits, axis=-1, keepdims=True))
    gate_probs = powers / jnp.sum(powers, axis=-1, keepdims=True)
    grad_logits = (
        gate_probs * (grad_probs - jnp.sum(grad_probs * gate_probs, axis=-1, keepdims=True))
    ).astype(BF16)
    grad_router_lift = (times_transposed(grad_logits, router_high) * own_sets).astype(BF16)
    grad_expert_in = (
        total[:, :D] + matmul(grad_logits, r.router_t[...]) + matmul(grad_router_lift, router_low)
    )
    _, unit, factor = normalize(hidden, gain_two, shift_two)
    grad_rows = grad_output + normalize_back(grad_expert_in, unit, factor, gain_two)
    r.grad_hidden[...] = grad_rows
    grad_attended = grad_rows.astype(BF16)
    grad_mixing_lift = (times_transposed(grad_attended, mixing_high) * own_sets).astype(BF16)
    grad_heads = (
        matmul(grad_attended, r.mixing_all[...]) + matmul(grad_mixing_lift, mixing_low)
    ).astype(BF16)
    r.heads[...] = grad_heads.reshape(images, half, D)
    mix = r.head_mix[...]
    lane = lax.broadcasted_iota(jnp.int32, (D, 128), 1)
    head = lax.div(lax.broadcasted_iota(jnp.int32, (D, 128), 0), HD)
    ones = (lane == head).astype(F32).astype(BF16)
    delta_rows = split_sum(grad_heads.astype(F32) * mix.astype(F32), ones)
    r.delta[...] = delta_rows
    log_rows = r.logs[...]
    for i in range(images):
        part = slice(i * half, (i + 1) * half)
        pad = jnp.zeros((128 - half, 128), F32)
        turned = [
            jnp.concatenate([v[part], pad], axis=0).T[:HEADS] for v in (log_rows, delta_rows)
        ]
        row = 0
        for rest, number in zip(turned, (3, 2)):
            for _ in range(number):
                top = rest.astype(BF16)
                r.stats[i, row : row + HEADS, :] = top
                rest = rest - top.astype(F32)
                row += HEADS

    def heads_slot(ctx, tp):
        at = pl.multiple_of((ctx * place.tp_size + tp) * half, 16)
        return r.heads_all.at[:, pl.ds(at, half), :]

    chain = Chain(
        place, wire, [r.heads, r.stats],
        [heads_slot, lambda ctx, tp: r.stats_all.at[ctx * place.tp_size + tp]],
        [True, True], True,
    )
    chain.start()

    def spread_start(values, got):
        rows = got.shape[1]
        copies = []
        for k, (dp, tp) in enumerate(place.peers):
            at = pl.ds(pl.multiple_of((dp * place.tp_size + tp) * rows, 16), rows)
            copy = wire.copy(values.at[at], got.at[k], {"dp": dp, "tp": tp})
            copy.start()
            copies.append(copy)
        return copies

    def spread_end(copies, values, got, total):
        rows = got.shape[1]
        for copy in copies:
            copy.wait()
        added = values[pl.ds(pl.multiple_of(place.me * rows, 16), rows), :].astype(F32)
        for k in range(plane - 1):
            added = added + got[k].astype(F32)
        total[...] = added.astype(BF16).reshape(total.shape)

    def put_tiles(target, products):
        tile = 0
        for product in products:
            for n in range(product.shape[1] // 128):
                target[tile * WIDTH : (tile + 1) * WIDTH, :] = product[
                    :, n * 128 : (n + 1) * 128
                ].astype(BF16)
                tile += 1
        if tile * WIDTH < target.shape[0]:
            target[tile * WIDTH :, :] = jnp.zeros(
                (target.shape[0] - tile * WIDTH, 128), BF16
            )

    wide_logits = jnp.concatenate(
        [grad_logits, jnp.zeros((count, 128 - EXPERTS), BF16)], axis=1
    )
    put_tiles(
        r.early,
        (
            inner_rows(grad_mixing_lift, mix),
            inner_rows(r.mixing_lift[...], grad_attended),
            inner_rows(grad_router_lift, rows),
            inner_rows(router_lift, wide_logits),
        ),
    )
    early_spread = spread_start(r.early, r.early_got)
    second_swap.wait()
    r.second_sum[...] = add_rounded(r.second[place.tp], r.second_got[...])
    send_end(second_at)
    go_first((last, FINAL), (last - 1, SENT), (last - 2, ONWARD))
    chain.step(1)
    go_first((last - 3, DONE), (last, SENT))
    chain.step(2)
    go(second_at, SUM)
    go_first((last - 1, ONWARD))
    chain.step(3)
    spread_end(early_spread, r.early, r.early_got, r.early_sum)
    send_end(early_at)
    go(second_at, FINAL)
    go_first((last - 2, DONE))
    chain.finish_own()
    for s in range(1, chain.steps + 1):
        chain.landed(s)

    def heads_back(i, j):
        part = slice(i * half, (i + 1) * half)
        at = slice(j * 2 * HD, (j + 1) * 2 * HD)
        keys_open = r.keys_open[i : i + 1, :] > 0
        own_open = jnp.concatenate([lives[i], lives[i]], axis=0) > 0
        found = jnp.concatenate(
            [r.stats_all[n, i][:, :half].astype(F32) for n in range(r.stats_all.shape[0])], axis=1
        )
        log_t = found[0:HEADS] + found[HEADS : 2 * HEADS] + found[2 * HEADS : 3 * HEADS]
        delta_t = found[3 * HEADS : 4 * HEADS] + found[4 * HEADS :]
        q_all, k_all, v_all = (r.joined[p, i, :, at] for p in range(3))
        g_all = r.heads_all[i, :, at]

        def column(values):
            return jnp.concatenate(
                [values[:, 2 * j : 2 * j + 1], values[:, 2 * j + 1 : 2 * j + 2]], axis=0
            )

        def across(values):
            return jnp.concatenate(
                [
                    jnp.broadcast_to(values[2 * j + n : 2 * j + n + 1, :], (half, values.shape[1]))
                    for n in range(2)
                ],
                axis=0,
            )

        q = stack_pair(r.joined[0, i, own, at], masks, scale)
        g = stack_pair(r.heads[i, :, at], masks)
        scores = jnp.where(keys_open, times_transposed(q, k_all), MASKED)
        probs = jnp.exp(scores - column(r.logs[part]))
        grad_probs_att = times_transposed(g, v_all)
        grad_scores = (probs * (grad_probs_att - column(r.delta[part]))).astype(BF16)
        r.grads[0, part, at] = (join_pair(matmul(grad_scores, k_all), masks) * scale).astype(BF16)
        k = stack_pair(r.joined[1, i, own, at], masks, scale)
        v = stack_pair(r.joined[2, i, own, at], masks)
        scores = jnp.where(own_open, times_transposed(k, q_all), MASKED)
        probs = jnp.exp(scores - across(log_t))
        grad_probs_att = times_transposed(v, g_all)
        grad_scores = (probs * (grad_probs_att - across(delta_t))).astype(BF16)
        r.grads[1, part, at] = (join_pair(matmul(grad_scores, q_all), masks) * scale).astype(BF16)
        r.grads[2, part, at] = join_pair(matmul(probs.astype(BF16), g_all), masks).astype(BF16)

    for i in range(images):
        for j in range(HEADS // 2):
            heads_back(i, j)
        if i == 0:
            go(early_at, SUM)
            go(second_at, SENT)
            go_first((last, ONWARD), (last - 1, DONE))
    go(early_at, FINAL)
    lift = times_transposed(r.grads[0], high(0))
    into = times_transposed(r.grads[0], r.weights_all[0])
    for p in range(1, 3):
        lift = lift + times_transposed(r.grads[p], high(p))
        into = into + times_transposed(r.grads[p], r.weights_all[p])
    lift = (lift * own_sets).astype(BF16)
    lift_in = jnp.concatenate([r.lift_all[i, own, :] for i in range(images)], axis=0)
    put_tiles(
        r.late,
        [inner_rows(lift_in, r.grads[p]) for p in range(3)]
        + [inner_rows(lift, r.own_in[...].reshape(count, D))],
    )
    late_spread = spread_start(r.late, r.late_got)
    go(second_at, ONWARD)
    into = into + matmul(lift, attend_low)
    flat = jnp.concatenate([r.tokens_all[i, own, :] for i in range(images)], axis=0).astype(F32)
    _, unit, factor = normalize(flat, gain_one, shift_one)
    result = r.grad_hidden[...] + normalize_back(into, unit, factor, gain_one)
    r.grad_own[...] = result.astype(BF16).reshape(images, half, D)
    for copy in returns[1]:
        copy.wait_recv()
    total = r.hidden[...]
    for k in range(r.received.shape[0]):
        total = total + r.received[k, :, CRITICAL:].astype(F32)
    r.out_own[...] = total.astype(BF16).reshape(images, half, D)
    outs = []
    for values, gathered in ((r.out_own, r.out_all), (r.grad_own, r.grad_all)):
        spot = gathered.at[:, pl.ds(start, half), :]
        outs.append(wire.copy(values, spot, {"tp": place.other_tp}))
        outs.append(wire.near(values, spot))
    spread_end(late_spread, r.late, r.late_got, r.late_sum)
    send_end(late_at)
    for copy in outs:
        copy.start()
    go(early_at, SENT)
    go_first((last, DONE))
    go(late_at, SUM)
    go(second_at, DONE)
    go(late_at, FINAL)
    go(early_at, ONWARD)
    go(late_at, SENT)
    go(early_at, DONE)
    for k in range(len(chunks)):
        go(k, DONE)

    @pl.when(place.is_end)
    def _():
        for flow in flows:
            flow["outer"].wait_send()
            flow["inner"].wait_send()

    @pl.when(place.is_mid)
    def _():
        for flow in flows:
            for name in ("cross", "back", "share", "pass_on"):
                flow[name].wait_send()

    for spread in spreads:
        spread.finish()
    for spread in [weights, mixing, numbers, router, cotangents, expert_rows] + spreads:
        spread.drain()
    tokens_chain.drain()
    chain.drain()
    for copy in late_sends:
        copy.wait_send()
    for copy in outs:
        copy.wait()
    assert not pending


def run_layer(sizes, **inputs):
    dp, ctx, tp = sizes
    assert ctx == 4 and tp == 2
    plane, chips = dp * tp, dp // 2
    images, block = inputs["tokens"].shape[:2]
    assert images == 2
    half = block // tp
    count, seq, all_images = images * half, ctx * block, dp * images
    experts, _, hidden = inputs["up_weight"].shape
    rows, lanes = inputs["mixing"].shape
    slots = experts * SLOTS
    sent = CRITICAL + D
    early_rows = small_rows(3 * (D // 128) + 1, plane)
    late_rows = small_rows(4 * (D // 128), plane)
    second = (2, experts, WIDTH, D // tp)
    full = dict(
        first=(experts, 2, WIDTH, hidden),
        second=second,
        early=(2, early_rows // 2, 128),
        late=(2, late_rows // 2, 128),
    )
    cut = {name: shape[1:] for name, shape in full.items()}
    cut["first"] = (experts, WIDTH, hidden)
    outputs = {name + "_all": (dp, tp) + shape for name, shape in full.items()}
    outputs.update(out_all=(images, block, D), grad_all=(images, block, D))
    narrow = dict(
        tokens_all=(images, seq, D),
        weights_all=(3, dp * rows, tp * lanes),
        mixing_all=(dp * rows, tp * lanes),
        router_all=(dp,) + inputs["router"].shape,
        router_t=(EXPERTS, D),
        cot_all=(all_images, block, D),
        rows_all=(all_images, block, D),
        v_attend_low=(SETS, RANK, D),
        v_attend_high=(SETS, 3, RANK, D),
        v_mixing_low=(SETS, RANK, D),
        v_mixing_high=(SETS, RANK, D),
        v_router_low=(SETS, RANK, D),
        v_router_high=(SETS, RANK, EXPERTS),
        v_first_a=(experts, SETS, RANK, D),
        v_first_b=(experts, SETS, RANK, hidden),
        v_second_a=(experts, SETS, RANK, hidden),
        v_second_b=(experts, SETS, RANK, D),
        v_up=(experts, D, hidden),
        v_down=(experts, hidden, D),
        lift_all=(images, seq, WIDTH),
        joined=(3, images, seq, D),
        own_in=(images, half, D),
        head_mix=(count, D),
        mixing_lift=(count, WIDTH),
        expert_in=(images, half, D),
        table=(all_images, slots, block),
        grad_slots=(experts, all_images * SLOTS, D),
        rows_in=(experts, all_images * SLOTS, D),
        payload=(all_images, slots, sent),
        partial=(2, chips, tp, count, sent),
        from_sibling=(chips, tp, count, sent),
        received=(chips * tp, count, sent),
        first=full["first"],
        second=(tp,) + second,
        second_got=second,
        second_sum=second,
        early=(plane * early_rows, 128),
        late=(plane * late_rows, 128),
        early_got=(plane - 1, early_rows, 128),
        late_got=(plane - 1, late_rows, 128),
        early_sum=full["early"],
        late_sum=full["late"],
        heads=(images, half, D),
        stats=(images, 5 * HEADS, 128),
        heads_all=(images, seq, D),
        stats_all=(ctx * tp, images, 5 * HEADS, 128),
        grads=(3, count, D),
        out_own=(images, half, D),
        grad_own=(images, half, D),
    )
    for name in full:
        narrow[name + "_end"] = narrow[name + "_final"] = full[name]
        narrow[name + "_mid"] = narrow[name + "_stage"] = cut[name]
    wide = dict(
        logs=(count, 128),
        delta=(count, 128),
        hidden=(count, D),
        grad_hidden=(count, D),
        gates=(experts, all_images * SLOTS, 128),
        slot_sets=(all_images * SLOTS, WIDTH),
        keys_open=(images, seq),
    )
    integers = dict(
        ints=(images, 8, block),
        ints_all=(all_images, 8, block),
        ctx_ints=(ctx, images, 8, block),
    )
    scratch = {}
    for shapes, dtype in ((narrow, BF16), (wide, F32), (integers, jnp.int32)):
        for name, shape in shapes.items():
            scratch[name] = pltpu.VMEM(shape, dtype)
    chunks = experts + 3
    remote = (
        2 * Chain.remote(ctx, 2)
        + (3 + chunks) * Spread.remote(sizes)
        + 3 * Spread.remote(sizes, False)
        + 6 * chunks
        + 2
        + 2 * (chips * tp - 1)
        + 2 * (plane - 1)
        + 2
    )
    scratch["send"] = pltpu.SemaphoreType.DMA((remote,))
    scratch["recv"] = pltpu.SemaphoreType.DMA((remote,))
    scratch["local"] = pltpu.SemaphoreType.DMA((7 + 6 * experts + 6 + chunks + 2 + 2,))
    kinds = dict(
        adapter_set=IN_SMEM, image_mask=IN_SMEM, gains=IN_VMEM, routes_t=IN_VMEM,
        slots_t=IN_VMEM, token_mask=IN_VMEM,
    )
    names = tuple(inputs) + tuple(outputs) + tuple(scratch)
    made = pl.pallas_call(
        functools.partial(layer_kernel, sizes, names),
        out_shape=tuple(jax.ShapeDtypeStruct(shape, BF16) for shape in outputs.values()),
        in_specs=[kinds.get(name, ANY) for name in inputs],
        out_specs=(ANY,) * len(outputs),
        scratch_shapes=tuple(scratch.values()),
        compiler_params=pltpu.CompilerParams(
            collective_id=0, has_side_effects=True, vmem_limit_bytes=62 << 20
        ),
    )(*inputs.values())
    return dict(zip(outputs, made))


def assemble_kernel(
    first, second, early, late, up, down_t, narrow_t, narrow,
    attend_down, attend_up, mixing_down, mixing_up, router_down, router_up,
):
    lanes, part = first.shape[-1], second.shape[-1]
    for tp in range(first.shape[1]):
        for half, out in ((0, up), (1, down_t)):
            out[:, 0, :, tp * lanes : (tp + 1) * lanes] = (
                first[0, tp, 0, half].astype(F32).reshape(SETS, RANK, lanes)
            )
        for half, out in ((0, narrow_t), (1, narrow)):
            out[:, 0, :, tp * part : (tp + 1) * part] = (
                second[0, tp, half, 0].astype(F32).reshape(SETS, RANK, part)
            )

    @pl.when(pl.program_id(0) == 0)
    def _():
        def tile(small, k):
            return small[k * WIDTH : (k + 1) * WIDTH, :].astype(F32).reshape(SETS, RANK, 128)

        count = D // 128
        for p in range(3):
            for k in range(count):
                attend_up[:, p, :, k * 128 : (k + 1) * 128] = tile(late, p * count + k)
        for k in range(count):
            attend_down[:, :, k * 128 : (k + 1) * 128] = tile(late, 3 * count + k)
        for p, out in enumerate((mixing_down, mixing_up, router_down)):
            for k in range(count):
                out[:, :, k * 128 : (k + 1) * 128] = tile(early, p * count + k)
        router_up[...] = tile(early, 3 * count)[:, :, :EXPERTS]


def assemble(first, second, early, late):
    dp, tp, experts, _, width, lanes = first.shape
    part = second.shape[-1]

    def split(e):
        return lax.div(e, experts), lax.rem(e, experts)

    def expert_out(size):
        return (
            jax.ShapeDtypeStruct((SETS, EXPERTS, RANK, size), F32),
            pl.BlockSpec((SETS, 1, RANK, size), lambda e: (0, e, 0, 0)),
        )

    def whole_out(*shape):
        return (
            jax.ShapeDtypeStruct(shape, F32),
            pl.BlockSpec(shape, lambda e: (0,) * len(shape)),
        )

    outs = (
        [expert_out(FF)] * 2
        + [expert_out(D)] * 2
        + [whole_out(SETS, RANK, D), whole_out(SETS, 3, RANK, D)]
        + [whole_out(SETS, RANK, D)] * 3
        + [whole_out(SETS, RANK, EXPERTS)]
    )
    return pl.pallas_call(
        assemble_kernel,
        grid=(EXPERTS,),
        out_shape=[out[0] for out in outs],
        in_specs=[
            pl.BlockSpec(
                (1, tp, 1, 2, width, lanes), lambda e: (split(e)[0], 0, split(e)[1], 0, 0, 0)
            ),
            pl.BlockSpec(
                (1, tp, 2, 1, width, part), lambda e: (split(e)[0], 0, 0, split(e)[1], 0, 0)
            ),
            pl.BlockSpec(early.shape, lambda e: (0, 0)),
            pl.BlockSpec(late.shape, lambda e: (0, 0)),
        ],
        out_specs=[out[1] for out in outs],
        compiler_params=pltpu.CompilerParams(vmem_limit_bytes=32 << 20),
    )(first, second, early, late)


def per_device(
    sizes,
    tokens,
    cotangent,
    routes,
    slot_index,
    token_mask,
    image_mask,
    adapter_set,
    first_gain,
    first_shift,
    second_gain,
    second_shift,
    attend_weight,
    mixing_weight,
    router_weight,
    expand_weight,
    shrink_weight,
    attend_down,
    attend_up,
    mixing_down,
    mixing_up,
    router_down,
    router_up,
    expand_down,
    expand_up,
    shrink_down,
    shrink_up,
):
    def flipped(values):
        return jnp.swapaxes(values, -1, -2)

    made = run_layer(
        sizes,
        tokens=tokens,
        cotangent=cotangent,
        weights=jnp.transpose(attend_weight, (1, 0, 2)),
        mixing=mixing_weight,
        router=flipped(router_weight),
        routes_t=flipped(routes),
        slots_t=flipped(slot_index),
        token_mask=token_mask,
        image_mask=image_mask,
        adapter_set=adapter_set,
        gains=jnp.stack([first_gain, first_shift, second_gain, second_shift]),
        up_weight=expand_weight,
        down_weight=shrink_weight,
        attend_low=flipped(attend_down),
        attend_high=jnp.transpose(attend_up, (0, 2, 1, 3)),
        mixing_low=flipped(mixing_down),
        mixing_high=mixing_up,
        router_low=flipped(router_down),
        router_high=router_up,
        first_a=flipped(expand_down),
        first_b=expand_up,
        second_a=flipped(shrink_down),
        second_b=shrink_up,
    )
    wide = assemble(
        made["first_all"],
        made["second_all"],
        made["early_all"].reshape(-1, 128),
        made["late_all"].reshape(-1, 128),
    )
    return (
        made["out_all"],
        made["grad_all"],
        flipped(wide[4]),
        jnp.transpose(wide[5], (0, 2, 1, 3)),
        flipped(wide[6]),
        wide[7],
        flipped(wide[8]),
        wide[9],
        flipped(wide[2]),
        wide[0],
        flipped(wide[1]),
        wide[3],
    )


def solution(mesh):
    sizes = (mesh.shape["dp"], mesh.shape["ctx"], mesh.shape["tp"])
    tokens_spec = P("dp", "ctx", None)
    in_specs = (
        (tokens_spec,) * 4
        + (P("dp", "ctx"), P("dp"), P("dp"))
        + (P(),) * 4
        + (P("dp", None, "tp"), P("dp", "tp"), P("dp", None))
        + (P("dp", None, "tp"), P("dp", "tp", None))
        + (P(),) * 10
    )
    out_specs = (tokens_spec,) * 2 + (P(),) * 10
    return jax.shard_map(
        functools.partial(per_device, sizes),
        mesh=mesh,
        in_specs=in_specs,
        out_specs=out_specs,
        check_vma=False,
    )
```

time: 857 us -> 206 us (0.24); the launches traced: 845 us -> 206 us
  waiting for transfers between devices: 490 us -> 0 us
  Pallas kernels: 0 us -> 196 us
  blocking collectives: 131 us -> 0 us
  local copies, waits for them, and re-layouts: 93.5 us -> 8.31 us
  matrix products: 70.4 us -> 0 us
  starting transfers between devices: 27.3 us -> 0 us
  other arithmetic: 16.8 us -> 1.34 us
  between operations: 16.1 us -> 0.68 us
    psum x4 -> x0, waiting for transfers between devices: 442 us -> none  [the longest x1 346 us: per_device(): lax.psum((full_attend_down, full_attend_up, full_mixing_down, full_mixing...]
    pallas_call x0 -> x2, Pallas kernels: none -> 196 us  [the longest x1 186 us: run_layer(): pl.pallas_call(functools.partial(layer_kernel, sizes, names), out_shape=t...]
    all_gather x6 -> x0, blocking collectives: 81 us -> none  [the longest x1 24.5 us: per_device(): lax.all_gather(value_block, 'ctx', axis=1, tiled=True)]
    dot_general x58 -> x0, matrix products: 70.4 us -> none  [the longest x1 11.4 us: expert_forward(): jnp.einsum('secr,erf->secf', lifted, first_b, preferred_element_type=SING...]
    psum x2 -> x0, blocking collectives: 49.8 us -> none  [the longest x1 43.3 us: per_device(): lax.psum((full_attend_down, full_attend_up, full_mixing_down, full_mixing...]
    unnamed x201 -> x14, local copies, waits for them, and re-layouts: 41.6 us -> 8.31 us
    all_to_all x5 -> x0, waiting for transfers between devices: 29.2 us -> none  [the longest x1 10.2 us: per_device(): lax.all_to_all(grad_send, 'dp', split_axis=1, concat_axis=0, tiled=True)]
    all_to_all x5 -> x0, starting transfers between devices: 26.9 us -> none  [the longest x1 6.56 us: per_device(): lax.all_to_all(set_values, 'dp', split_axis=1, concat_axis=0, tiled=True)]
  transfers between devices with their start and end apart: 11 -> 0, of which waited for: 8 -> 0; matrix products, arithmetic and copies ran while one was open for 7% -> 0% of each run, Pallas kernels for 0% -> 0%
where the time goes in v1:
time: 206 us
  Pallas kernels  196 us (95%)
  local copies, waits for them, and re-layouts  8.31 us (4%)
    pallas_call x1, Pallas kernels, run_layer(): pl.pallas_call(functools.partial(layer_kernel, sizes, names), out_shape=t...  186 us
    pallas_call x1, Pallas kernels, assemble(): pl.pallas_call(assemble_kernel, grid=(EXPERTS,), out_shape=[out[0] for ou...  10.1 us
    unnamed x14, local copies, waits for them, and re-layouts  8.31 us

profile of v1, /device:TPU:1, one launch (start us, length us, event | category | flops | bytes accessed | tf_op | source)
XLA Modules:
  0.0 206.2 jit_solution(501524100428768423)
XLA Ops:
  0.6 1.3 pad_maximum_fusion.refs_10_
  2.0 185.8 %shard_map.337 = (bf16[4,2,4,2,64,1024]{5,4,3,2,1,0:T(8,128)(2,1)}, bf16[4,2,2,4,64,256]{5,4,3,2,1,0:T(8,128)(2,1)}, bf16[4,2,2,56,128]{4,3,2,1,0:T(8,128)(2,1)}...) custom-call(bf16[2,160,512]{2,1,0:T(8,128)(2,1)} %refs_0_.1, ...), custom_call_target="tpu_custom_call" | custom-call | tf_op jit(solution)/shard_map/pallas_call | solution.py:1175
  187.8 0.0 copy-start
  187.8 3.4 %copy-done = bf16[4,2,4,2,64,1024]{5,4,3,2,1,0:T(8,128)(2,1)S(1)} copy-done((bf16[4,2,4,2,64,1024]{5,4,3,2,1,0:T(8,128)(2,1)S(1)}, bf16[4,2,4,2,64,1024]{5,4,3,2,1,0:T(8,128)(2,1)}, u32[]{:S(2)}) %copy-start) | copy-done | bytes 8388632
  191.1 0.0 copy-start.1
  191.1 1.6 copy-done.1
  192.7 0.0 copy-start.2
  192.7 0.9 copy-done.2
  193.7 0.0 copy-start.3
  193.7 0.9 copy-done.3
  194.6 0.0 copy-start.5
  194.6 0.0 copy-start.4
  194.6 10.1 %shard_map.338 = (f32[4,16,16,2048]{3,2,1,0:T(8,128)}, f32[4,16,16,2048]{3,2,1,0:T(8,128)}, f32[4,16,16,512]{3,2,1,0:T(8,128)}, f32[4,16,16,512]{3,2,1,0:T(8,128...) custom-call(bf16[4,2,4,2,64,1024]{5,4,3,2,1,0:T(8,128)(2,1)S(1)} %co, ...), custom_call_target="tpu_custom_call" | custom-call | tf_op jit(solution)/shard_map/pallas_call | solution.py:1246
  204.7 0.0 copy-done.5
  204.7 0.7 copy.40
  205.4 0.0 copy-done.4
  205.4 0.7 copy.41
Async XLA Ops:
  187.8 3.4 %copy-start = (bf16[4,2,4,2,64,1024]{5,4,3,2,1,0:T(8,128)(2,1)S(1)}, bf16[4,2,4,2,64,1024]{5,4,3,2,1,0:T(8,128)(2,1)}, u32[]{:S(2)}) copy-start(bf16[4,2,4,2,64,1024]{5,4,3,2,1,0:T(8,128)(2,1)} %get-tuple-element.30.first) | copy-start | bytes 25165828
  191.1 1.6 copy-start.1
  192.7 0.9 copy-start.2
  193.7 0.9 copy-start.3
  194.6 10.1 %copy-start.5 = (bf16[2,160,512]{2,1,0:T(8,128)(2,1)S(1)}, bf16[2,160,512]{2,1,0:T(8,128)(2,1)}, u32[]{:S(2)}) copy-start(bf16[2,160,512]{2,1,0:T(8,128)(2,1)} %get-tuple-element.56) | copy-start | bytes 983044
  194.6 10.8 %copy-start.4 = (bf16[2,160,512]{2,1,0:T(8,128)(2,1)S(1)}, bf16[2,160,512]{2,1,0:T(8,128)(2,1)}, u32[]{:S(2)}) copy-start(bf16[2,160,512]{2,1,0:T(8,128)(2,1)} %get-tuple-element.57) | copy-start | bytes 983044

commit v2 on v1

--- a/solution.py
+++ b/solution.py
@@ -23,6 +23,7 @@
 SET_ROW = LIVE_ROW + 1
 CRITICAL = D + 128
 EXPERT_ROWS = 256
+ASSEMBLED = 2
 
 EPSILON = 1e-06
 MASKED = -1e30
@@ -104,6 +105,30 @@
 def join_pair(rows, masks):
     half = rows.shape[0] // 2
     return rows[:half] * masks[0] + rows[half:] * masks[1]
+
+
+SUM, SENT, ONWARD, DONE = range(1, 5)
+E0, E1, E2, E3, SECOND, EARLY, LATE = range(-7, 0)
+SCHEDULE = (
+    (),
+    ((E0, SUM),),
+    ((E1, SUM),),
+    ((E0, SENT), (E2, SUM), (E1, SENT)),
+    ((E0, ONWARD), (E3, SUM)),
+    ((E2, SENT), (E1, ONWARD)),
+    ((E0, DONE), (SECOND, SUM)),
+    ((E3, SENT), (E2, ONWARD)),
+    ((E1, DONE),),
+    ((SECOND, SENT),),
+    ((EARLY, SUM), (E3, ONWARD)),
+    ((E2, DONE),),
+    ((SECOND, ONWARD),),
+    ((EARLY, SENT),),
+    (
+        (E3, DONE), (LATE, SUM), (EARLY, ONWARD), (SECOND, DONE), (LATE, SENT), (EARLY, DONE),
+        (LATE, ONWARD), (LATE, DONE),
+    ),
+)
 
 
 def small_rows(tiles, plane):
@@ -152,7 +177,8 @@
         self.is_end = jnp.logical_not(self.is_mid)
         self.inner = lax.div(self.ctx, 2)
         self.partner = jnp.where(self.is_mid, self.inner * 3, 1 + self.inner)
-        self.other_mid = 2 - self.inner
+        self.far_mid = 2 - self.inner
+        self.far_end = 3 - 3 * self.inner
         self.peers = []
         for k in range(1, self.plane):
             peer = lax.rem(self.me + k, self.plane)
@@ -181,17 +207,18 @@
             pl.semaphore_signal(
                 barrier, inc=1, device_id={"dp": dp, "tp": tp}, device_id_type=MESH
             )
-        pl.semaphore_signal(
-            barrier, inc=1, device_id={"ctx": self.partner}, device_id_type=MESH
-        )
+        for ctx in (self.partner, self.far_mid):
+            pl.semaphore_signal(barrier, inc=1, device_id={"ctx": ctx}, device_id_type=MESH)
 
         @pl.when(self.is_mid)
         def _():
             pl.semaphore_signal(
-                barrier, inc=1, device_id={"ctx": self.other_mid}, device_id_type=MESH
+                barrier, inc=1, device_id={"ctx": self.far_end}, device_id_type=MESH
             )
 
-        pl.semaphore_wait(barrier, self.plane + jnp.where(self.is_mid, 1, 0))
+    def met(self):
+        barrier = pltpu.get_barrier_semaphore()
+        pl.semaphore_wait(barrier, self.plane + 1 + jnp.where(self.is_mid, 1, 0))
 
 
 class Spread:
@@ -282,8 +309,12 @@
             self.left[s] = [
                 wire.copy(a if s == 1 else b, b, to_left) for a, b in zip(sources, ahead)
             ]
-            self.over_right[s] = [wire.copy(b, b, to_tp) for b, o in zip(got_right, over) if o]
-            self.over_left[s] = [wire.copy(b, b, to_tp) for b, o in zip(got_left, over) if o]
+            self.over_right[s] = {
+                k: wire.copy(b, b, to_tp) for k, b in enumerate(got_right) if over[k]
+            }
+            self.over_left[s] = {
+                k: wire.copy(b, b, to_tp) for k, b in enumerate(got_left) if over[k]
+            }
 
     def sends_right(self, s):
         return jnp.logical_and(self.place.ctx >= s - 1, self.place.ctx < self.steps)
@@ -310,10 +341,12 @@
     def step(self, s):
         def passed(got, over, sends):
             def run():
-                self.all_of(got[s], "wait_recv")
-                if s < self.steps:
-                    pl.when(sends(s + 1))(lambda: self.all_of(got[s + 1], "start"))
-                self.all_of(over[s], "start")
+                for k, copy in enumerate(got[s]):
+                    copy.wait_recv()
+                    if s < self.steps:
+                        pl.when(sends(s + 1))(got[s + 1][k].start)
+                    if k in over[s]:
+                        over[s][k].start()
 
             return run
 
@@ -321,8 +354,8 @@
         pl.when(self.gets_left(s))(passed(self.left, self.over_left, self.sends_left))
 
     def landed(self, s):
-        pl.when(self.gets_right(s))(lambda: self.all_of(self.over_right[s], "wait_recv"))
-        pl.when(self.gets_left(s))(lambda: self.all_of(self.over_left[s], "wait_recv"))
+        pl.when(self.gets_right(s))(lambda: self.all_of(self.over_right[s].values(), "wait_recv"))
+        pl.when(self.gets_left(s))(lambda: self.all_of(self.over_left[s].values(), "wait_recv"))
 
     def finish_own(self):
         self.all_of(self.own, "wait_recv")
@@ -331,8 +364,8 @@
     def drain(self):
         self.all_of(self.own, "wait_send")
         for s in range(1, self.steps + 1):
-            pl.when(self.gets_right(s))(lambda: self.all_of(self.over_right[s], "wait_send"))
-            pl.when(self.gets_left(s))(lambda: self.all_of(self.over_left[s], "wait_send"))
+            pl.when(self.gets_right(s))(lambda: self.all_of(self.over_right[s].values(), "wait_send"))
+            pl.when(self.gets_left(s))(lambda: self.all_of(self.over_left[s].values(), "wait_send"))
             pl.when(self.sends_right(s))(lambda: self.all_of(self.right[s], "wait_send"))
             pl.when(self.sends_left(s))(lambda: self.all_of(self.left[s], "wait_send"))
 
@@ -370,12 +403,65 @@
             if name in pending:
                 pending.pop(name).wait()
 
+    place.greet()
     whole = pl.ds(pl.multiple_of(place.ctx * block, 16), block)
     load("tokens", r.tokens, r.tokens_all.at[:, whole, :])
     for name in (
         "attend_low", "attend_high", "mixing_low", "mixing_high", "router_low", "router_high",
     ):
         load(name, getattr(r, name), getattr(r, "v_" + name))
+    r.ints[:, 0:TOP, :] = r.routes_t[...]
+    r.ints[:, TOP : 2 * TOP, :] = r.slots_t[...]
+    lane_set = lax.div(lax.broadcasted_iota(jnp.int32, (1, WIDTH), 1), RANK)
+    picks = []
+    for i in range(images):
+        r.ints[i, LIVE_ROW : LIVE_ROW + 1, :] = r.token_mask[i : i + 1, :] * r.image_mask[i]
+        r.ints[i, SET_ROW:, :] = jnp.full((8 - SET_ROW, block), r.adapter_set[i], jnp.int32)
+        picks.append((lane_set == r.adapter_set[i]).astype(F32))
+    gain_one, shift_one = r.first_gain[...], r.first_shift[...]
+    gain_two, shift_two = r.second_gain[...], r.second_shift[...]
+
+    place.met()
+
+    rows, lanes = r.mixing.shape
+
+    def at_rows(dp):
+        return pl.ds(pl.multiple_of(dp * rows, 16), rows)
+
+    def at_lanes(tp):
+        return pl.ds(pl.multiple_of(tp * lanes, 128), lanes)
+
+    def token_slot(i, ctx, tp):
+        at = pl.multiple_of(ctx * block + tp * half, 16)
+        return r.tokens_all.at[i, pl.ds(at, half), :]
+
+    tokens_chain = Chain(
+        place, wire,
+        [r.tokens.at[i, pl.ds(start, half), :] for i in range(images)] + [r.ints],
+        [functools.partial(token_slot, i) for i in range(images)]
+        + [lambda ctx, tp: r.ctx_ints.at[ctx]],
+        [True] * images + [False], False,
+    )
+    weights = Spread(
+        place, wire, r.weights, lambda dp, tp: r.weights_all.at[:, at_rows(dp), at_lanes(tp)]
+    )
+    mixing = Spread(
+        place, wire, r.mixing, lambda dp, tp: r.mixing_all.at[at_rows(dp), at_lanes(tp)]
+    )
+    numbers = Spread(
+        place, wire, r.ints, lambda dp, tp: r.ints_all.at[pl.ds(dp * 2, 2)], over_tp=False
+    )
+    router = Spread(place, wire, r.router, lambda dp, tp: r.router_all.at[dp], over_tp=False)
+    cotangents = Spread(
+        place, wire, r.cotangent, lambda dp, tp: r.cot_all.at[pl.ds(dp * 2, 2)], over_tp=False
+    )
+    r.ctx_ints[place.ctx] = r.ints[...]
+    tokens_chain.start()
+    weights.start()
+    numbers.start()
+    router.start()
+    mixing.start()
+    cotangents.start()
     wide = pl.ds(pl.multiple_of(place.tp * hidden_units, 128), hidden_units)
     for e in range(experts):
         load(("a_first", e), r.first_a.at[:, owned + e], r.v_first_a.at[e])
@@ -384,55 +470,6 @@
         load(("a_second", e), r.second_a.at[:, owned + e, :, wide], r.v_second_a.at[e])
         load(("b_second", e), r.second_b.at[:, owned + e], r.v_second_b.at[e])
         load(("down", e), r.down_weight.at[e], r.v_down.at[e])
-    r.ints[:, 0:TOP, :] = r.routes_t[...]
-    r.ints[:, TOP : 2 * TOP, :] = r.slots_t[...]
-    lane_set = lax.div(lax.broadcasted_iota(jnp.int32, (1, WIDTH), 1), RANK)
-    picks = []
-    for i in range(images):
-        r.ints[i, LIVE_ROW : LIVE_ROW + 1, :] = r.token_mask[i : i + 1, :] * r.image_mask[i]
-        r.ints[i, SET_ROW:, :] = jnp.full((8 - SET_ROW, block), r.adapter_set[i], jnp.int32)
-        picks.append((lane_set == r.adapter_set[i]).astype(F32))
-    gain_one, shift_one = r.gains[0:1, :], r.gains[1:2, :]
-    gain_two, shift_two = r.gains[2:3, :], r.gains[3:4, :]
-
-    place.greet()
-
-    rows, lanes = r.mixing.shape
-
-    def at_rows(dp):
-        return pl.ds(pl.multiple_of(dp * rows, 16), rows)
-
-    def at_lanes(tp):
-        return pl.ds(pl.multiple_of(tp * lanes, 128), lanes)
-
-    def token_slot(ctx, tp):
-        at = pl.multiple_of(ctx * block + tp * half, 16)
-        return r.tokens_all.at[:, pl.ds(at, half), :]
-
-    tokens_chain = Chain(
-        place, wire, [r.tokens.at[:, pl.ds(start, half), :], r.ints],
-        [token_slot, lambda ctx, tp: r.ctx_ints.at[ctx]], [True, False], False,
-    )
-    weights = Spread(
-        place, wire, r.weights, lambda dp, tp: r.weights_all.at[:, at_rows(dp), at_lanes(tp)]
-    )
-    mixing = Spread(
-        place, wire, r.mixing, lambda dp, tp: r.mixing_all.at[at_rows(dp), at_lanes(tp)]
-    )
-    numbers = Spread(
-        place, wire, r.ints, lambda dp, tp: r.ints_all.at[pl.ds(dp * 2, 2)], over_tp=False
-    )
-    router = Spread(place, wire, r.router, lambda dp, tp: r.router_all.at[dp], over_tp=False)
-    cotangents = Spread(
-        place, wire, r.cotangent, lambda dp, tp: r.cot_all.at[pl.ds(dp * 2, 2)], over_tp=False
-    )
-    r.ctx_ints[place.ctx] = r.ints[...]
-    tokens_chain.start()
-    weights.start()
-    numbers.start()
-    router.start()
-    mixing.start()
-    cotangents.start()
     weights.forward()
     tokens_chain.step(1)
     weights.diagonal()
@@ -504,6 +541,11 @@
             > 0
         )
 
+    def rows_slot(i, dp, tp):
+        at = pl.multiple_of(tp * half, 16)
+        return r.rows_all.at[dp * images + i, pl.ds(at, half), :]
+
+    expert_rows = []
     for i in range(images):
         r.keys_open[i : i + 1, :] = open_keys(i).astype(F32)
         token_rows = r.tokens_all[i, own, :].astype(F32)
@@ -531,13 +573,10 @@
         hidden = token_rows + times_transposed(mix, r.mixing_all[...]) + matmul(lift, mixing_high)
         r.hidden[part, :] = hidden
         r.expert_in[i] = normalize(hidden, gain_two, shift_two)[0].astype(BF16)
-
-    def rows_slot(dp, tp):
-        at = pl.multiple_of(tp * half, 16)
-        return r.rows_all.at[pl.ds(dp * 2, 2), pl.ds(at, half), :]
-
-    expert_rows = Spread(place, wire, r.expert_in, rows_slot, direct=True)
-    expert_rows.start()
+        expert_rows.append(
+            Spread(place, wire, r.expert_in.at[i], functools.partial(rows_slot, i), direct=True)
+        )
+        expert_rows[i].start()
 
     slots = experts * SLOTS
     cotangents.finish()
@@ -570,9 +609,11 @@
         fill_slots(i, r.grad_slots, matmul(hot, r.cot_all[i]).astype(BF16))
         return 0
 
-    lax.fori_loop(0, all_images, make_table, 0)
-    expert_rows.forward()
-    expert_rows.finish()
+    lax.fori_loop(0, all_images, make_table, 0, unroll=2)
+    for spread in expert_rows:
+        spread.forward()
+    for spread in expert_rows:
+        spread.finish()
 
     def dispatch(i, _):
         values = r.rows_all[i]
@@ -599,85 +640,73 @@
         r.slot_sets[at, :] = (lane == given[SET_ROW : SET_ROW + 1, 0:1]).astype(F32)
         return 0
 
-    lax.fori_loop(0, all_images, dispatch, 0)
+    lax.fori_loop(0, all_images, dispatch, 0, unroll=4)
 
     chunks = [
         (
-            r.first.at[e], r.first_end.at[e], r.first_mid.at[e], r.first_stage.at[e],
-            r.first_final.at[e],
+            r.first.at[e], r.first_got.at[e], r.first_final.at[e],
             functools.partial(lambda e, dp, tp: r.first_all.at[dp, tp, e], e),
         )
         for e in range(experts)
     ]
     chunks += [
-        (r.second_sum, r.second_end, r.second_mid, r.second_stage, r.second_final,
-         lambda dp, tp: r.second_all.at[dp, tp]),
-        (r.early_sum, r.early_end, r.early_mid, r.early_stage, r.early_final,
-         lambda dp, tp: r.early_all.at[dp, tp]),
-        (r.late_sum, r.late_end, r.late_mid, r.late_stage, r.late_final,
-         lambda dp, tp: r.late_all.at[dp, tp]),
+        (r.second_sum, r.second_in, r.second_final, lambda dp, tp: r.second_all.at[dp, tp]),
+        (r.early_sum, r.early_in, r.early_final, lambda dp, tp: r.early_all.at[dp, tp]),
+        (r.late_sum, r.late_in, r.late_final, lambda dp, tp: r.late_all.at[dp, tp]),
     ]
-    inner, outer_half = place.inner, 1 - place.inner
-    to_partner, to_mid = {"ctx": place.partner}, {"ctx": place.other_mid}
+    inner, outer = place.inner, 1 - place.inner
+    to_partner, to_far = {"ctx": place.partner}, {"ctx": place.far_mid}
     flows, spreads = [], []
-    for mine, end, mid, stage, final, slot in chunks:
+    for mine, got, final, slot in chunks:
         flows.append(
             dict(
-                outer=wire.copy(mine.at[outer_half], end.at[outer_half], to_partner),
-                inner=wire.copy(mine.at[inner], end.at[inner], to_partner),
-                cross=wire.copy(stage, mid, to_mid),
+                beside=wire.copy(mine.at[inner], got.at[0], to_partner),
+                across=wire.copy(mine.at[outer], got.at[1], to_far),
+                beyond=wire.copy(mine.at[outer], got.at[2], to_far),
                 back=wire.copy(final.at[inner], final.at[inner], to_partner),
-                share=wire.copy(final.at[inner], final.at[inner], to_mid),
-                pass_on=wire.copy(final.at[outer_half], final.at[outer_half], to_partner),
+                share=wire.copy(final.at[inner], final.at[inner], to_far),
+                away=wire.copy(final.at[inner], final.at[inner], {"ctx": place.far_end}),
             )
         )
         spreads.append(Spread(place, wire, final, slot))
 
-    def send_end(k):
+    def offer(k):
         @pl.when(place.is_end)
         def _():
-            flows[k]["outer"].start()
-            flows[k]["inner"].start()
-
-    def mid_first(k):
-        mine, end, mid, stage, final, slot = chunks[k]
+            flows[k]["beyond"].start()
+            flows[k]["beside"].start()
 
         @pl.when(place.is_mid)
         def _():
-            flows[k]["outer"].wait_recv()
-            stage[...] = add_rounded(mine[outer_half], end[outer_half])
-            flows[k]["cross"].start()
-
-    def mid_second(k):
-        mine, end, mid, stage, final, slot = chunks[k]
+            flows[k]["across"].start()
+
+    def total_half(k):
+        mine, got, final, slot = chunks[k]
 
         @pl.when(place.is_mid)
         def _():
-            flows[k]["inner"].wait_recv()
-            flows[k]["cross"].wait_recv()
-            final[inner] = add_rounded(mine[inner], end[inner], mid[...])
-            flows[k]["share"].start()
-            flows[k]["back"].start()
+            for name in ("beside", "across", "beyond"):
+                flows[k][name].wait_recv()
+            final[inner] = add_rounded(mine[inner], got[0], got[1], got[2])
+            for name in ("away", "share", "back"):
+                flows[k][name].start()
 
     def settle(k):
         @pl.when(place.is_mid)
         def _():
             flows[k]["share"].wait_recv()
-            flows[k]["pass_on"].start()
 
         @pl.when(place.is_end)
         def _():
             flows[k]["back"].wait_recv()
-            flows[k]["pass_on"].wait_recv()
+            flows[k]["away"].wait_recv()
 
         spreads[k].start()
 
     stages = (
-        mid_first, mid_second, settle,
-        lambda k: spreads[k].forward(), lambda k: spreads[k].diagonal(),
+        total_half, settle, lambda k: spreads[k].forward(), lambda k: spreads[k].diagonal(),
     )
     reached = [0] * len(chunks)
-    SUM, FINAL, SENT, ONWARD, DONE = range(1, 6)
     second_at, early_at, late_at = experts, experts + 1, experts + 2
 
     def go(k, stage):
@@ -685,10 +714,10 @@
             stages[reached[k]](k)
             reached[k] += 1
 
-    def go_first(*pairs):
-        for k, stage in pairs:
-            if k < experts:
-                go(k, stage)
+    def at_point(point):
+        for chunk, stage in SCHEDULE[point]:
+            if len(chunks) + chunk >= 0:
+                go(len(chunks) + chunk, stage)
 
     def run_expert(e):
         need(("a_first", e), ("b_first", e), ("up", e))
@@ -744,13 +773,16 @@
 
     for e in range(experts):
         run_expert(e)
-        send_end(e)
-        go_first(*((e - 1 - n, n + 1) for n in range(3) if e - 1 - n >= 0))
+        offer(e)
+        if e == experts - 2:
+            at_point(0)
+    at_point(1)
 
     second_swap = wire.copy(
         r.second.at[place.other_tp], r.second_got, {"tp": place.other_tp}
     )
     swap = wire.copy(r.partial.at[1 - place.core], r.from_sibling, {"dp": place.sibling})
+    second_swap.start()
 
     def combine(core):
         def run(chip, _):
@@ -768,6 +800,10 @@
     combine(1 - place.core)
     swap.start()
     combine(place.core)
+    at_point(2)
+    second_swap.wait()
+    r.second_sum[...] = add_rounded(r.second[place.tp], r.second_got[...])
+    offer(second_at)
     swap.wait_recv()
     returns = []
     for at in (slice(0, CRITICAL), slice(CRITICAL, CRITICAL + D)):
@@ -791,12 +827,8 @@
             else:
                 r.received[0, :, at] = both
         returns.append(copies)
-        if not at.start:
-            second_swap.start()
     late_sends = [swap] + returns[0] + returns[1]
-    last = experts - 1
-    go_first((last - 2, SENT), (last - 1, FINAL), (last, SUM))
-    go_first((last - 3, ONWARD))
+    at_point(3)
     for copy in returns[0]:
         copy.wait_recv()
 
@@ -861,14 +893,15 @@
                 rest = rest - top.astype(F32)
                 row += HEADS
 
-    def heads_slot(ctx, tp):
+    def heads_slot(i, ctx, tp):
         at = pl.multiple_of((ctx * place.tp_size + tp) * half, 16)
-        return r.heads_all.at[:, pl.ds(at, half), :]
+        return r.heads_all.at[i, pl.ds(at, half), :]
 
     chain = Chain(
-        place, wire, [r.heads, r.stats],
-        [heads_slot, lambda ctx, tp: r.stats_all.at[ctx * place.tp_size + tp]],
-        [True, True], True,
+        place, wire, [r.heads.at[i] for i in range(images)] + [r.stats],
+        [functools.partial(heads_slot, i) for i in range(images)]
+        + [lambda ctx, tp: r.stats_all.at[ctx * place.tp_size + tp]],
+        [True] * (images + 1), True,
     )
     chain.start()
 
@@ -917,23 +950,33 @@
         ),
     )
     early_spread = spread_start(r.early, r.early_got)
-    second_swap.wait()
-    r.second_sum[...] = add_rounded(r.second[place.tp], r.second_got[...])
-    send_end(second_at)
-    go_first((last, FINAL), (last - 1, SENT), (last - 2, ONWARD))
+    at_point(4)
     chain.step(1)
-    go_first((last - 3, DONE), (last, SENT))
+    at_point(5)
     chain.step(2)
-    go(second_at, SUM)
-    go_first((last - 1, ONWARD))
+    at_point(6)
     chain.step(3)
     spread_end(early_spread, r.early, r.early_got, r.early_sum)
-    send_end(early_at)
-    go(second_at, FINAL)
-    go_first((last - 2, DONE))
+    offer(early_at)
+    at_point(7)
     chain.finish_own()
     for s in range(1, chain.steps + 1):
         chain.landed(s)
+
+    def to_other(values, gathered):
+        spot = gathered.at[:, pl.ds(start, half), :]
+        copies = [wire.copy(values, spot, {"tp": place.other_tp}), wire.near(values, spot)]
+        for copy in copies:
+            copy.start()
+        return copies
+
+    for copy in returns[1]:
+        copy.wait_recv()
+    total = r.hidden[...]
+    for k in range(r.received.shape[0]):
+        total = total + r.received[k, :, CRITICAL:].astype(F32)
+    r.out_own[...] = total.astype(BF16).reshape(images, half, D)
+    layer_out = to_other(r.out_own, r.out_all)
 
     def heads_back(i, j):
         part = slice(i * half, (i + 1) * half)
@@ -981,11 +1024,8 @@
     for i in range(images):
         for j in range(HEADS // 2):
             heads_back(i, j)
-        if i == 0:
-            go(early_at, SUM)
-            go(second_at, SENT)
-            go_first((last, ONWARD), (last - 1, DONE))
-    go(early_at, FINAL)
+            if j % 2:
+                at_point(8 + 2 * i + j // 2)
     lift = times_transposed(r.grads[0], high(0))
     into = times_transposed(r.grads[0], r.weights_all[0])
     for p in range(1, 3):
@@ -999,59 +1039,41 @@
         + [inner_rows(lift, r.own_in[...].reshape(count, D))],
     )
     late_spread = spread_start(r.late, r.late_got)
-    go(second_at, ONWARD)
+    at_point(12)
     into = into + matmul(lift, attend_low)
     flat = jnp.concatenate([r.tokens_all[i, own, :] for i in range(images)], axis=0).astype(F32)
     _, unit, factor = normalize(flat, gain_one, shift_one)
     result = r.grad_hidden[...] + normalize_back(into, unit, factor, gain_one)
     r.grad_own[...] = result.astype(BF16).reshape(images, half, D)
-    for copy in returns[1]:
-        copy.wait_recv()
-    total = r.hidden[...]
-    for k in range(r.received.shape[0]):
-        total = total + r.received[k, :, CRITICAL:].astype(F32)
-    r.out_own[...] = total.astype(BF16).reshape(images, half, D)
-    outs = []
-    for values, gathered in ((r.out_own, r.out_all), (r.grad_own, r.grad_all)):
-        spot = gathered.at[:, pl.ds(start, half), :]
-        outs.append(wire.copy(values, spot, {"tp": place.other_tp}))
-        outs.append(wire.near(values, spot))
+    at_point(13)
+    tokens_out = to_other(r.grad_own, r.grad_all)
     spread_end(late_spread, r.late, r.late_got, r.late_sum)
-    send_end(late_at)
-    for copy in outs:
-        copy.start()
-    go(early_at, SENT)
-    go_first((last, DONE))
-    go(late_at, SUM)
-    go(second_at, DONE)
-    go(late_at, FINAL)
-    go(early_at, ONWARD)
-    go(late_at, SENT)
-    go(early_at, DONE)
+    offer(late_at)
+    at_point(14)
     for k in range(len(chunks)):
         go(k, DONE)
 
     @pl.when(place.is_end)
     def _():
         for flow in flows:
-            flow["outer"].wait_send()
-            flow["inner"].wait_send()
+            flow["beyond"].wait_send()
+            flow["beside"].wait_send()
 
     @pl.when(place.is_mid)
     def _():
         for flow in flows:
-            for name in ("cross", "back", "share", "pass_on"):
+            for name in ("across", "away", "share", "back"):
                 flow[name].wait_send()
 
     for spread in spreads:
         spread.finish()
-    for spread in [weights, mixing, numbers, router, cotangents, expert_rows] + spreads:
+    for spread in [weights, mixing, numbers, router, cotangents] + expert_rows + spreads:
         spread.drain()
     tokens_chain.drain()
     chain.drain()
     for copy in late_sends:
         copy.wait_send()
-    for copy in outs:
+    for copy in layer_out + tokens_out:
         copy.wait()
     assert not pending
 
@@ -1133,8 +1155,10 @@
         grad_own=(images, half, D),
     )
     for name in full:
-        narrow[name + "_end"] = narrow[name + "_final"] = full[name]
-        narrow[name + "_mid"] = narrow[name + "_stage"] = cut[name]
+        narrow[name + "_final"] = full[name]
+        narrow[name + "_in"] = (3,) + cut[name]
+    narrow["first_got"] = (experts, 3, WIDTH, hidden)
+    del narrow["first_in"]
     wide = dict(
         logs=(count, 128),
         delta=(count, 128),
@@ -1155,8 +1179,8 @@
             scratch[name] = pltpu.VMEM(shape, dtype)
     chunks = experts + 3
     remote = (
-        2 * Chain.remote(ctx, 2)
-        + (3 + chunks) * Spread.remote(sizes)
+        2 * Chain.remote(ctx, images + 1)
+        + (2 + images + chunks) * Spread.remote(sizes)
         + 3 * Spread.remote(sizes, False)
         + 6 * chunks
         + 2
@@ -1166,10 +1190,11 @@
     )
     scratch["send"] = pltpu.SemaphoreType.DMA((remote,))
     scratch["recv"] = pltpu.SemaphoreType.DMA((remote,))
-    scratch["local"] = pltpu.SemaphoreType.DMA((7 + 6 * experts + 6 + chunks + 2 + 2,))
+    scratch["local"] = pltpu.SemaphoreType.DMA((7 + 6 * experts + 5 + images + chunks + images + 1 + 2,))
     kinds = dict(
-        adapter_set=IN_SMEM, image_mask=IN_SMEM, gains=IN_VMEM, routes_t=IN_VMEM,
-        slots_t=IN_VMEM, token_mask=IN_VMEM,
+        adapter_set=IN_SMEM, image_mask=IN_SMEM, routes_t=IN_VMEM, slots_t=IN_VMEM,
+        token_mask=IN_VMEM, first_gain=IN_VMEM, first_shift=IN_VMEM, second_gain=IN_VMEM,
+        second_shift=IN_VMEM,
     )
     names = tuple(inputs) + tuple(outputs) + tuple(scratch)
     made = pl.pallas_call(
@@ -1186,19 +1211,21 @@
 
 
 def assemble_kernel(
-    first, second, early, late, up, down_t, narrow_t, narrow,
-    attend_down, attend_up, mixing_down, mixing_up, router_down, router_up,
+    first, second, early, late, out_in, grad_in,
+    up, down_t, narrow_t, narrow, attend_down, attend_up, mixing_down, mixing_up, router_down,
+    router_up, out, grad,
 ):
     lanes, part = first.shape[-1], second.shape[-1]
-    for tp in range(first.shape[1]):
-        for half, out in ((0, up), (1, down_t)):
-            out[:, 0, :, tp * lanes : (tp + 1) * lanes] = (
-                first[0, tp, 0, half].astype(F32).reshape(SETS, RANK, lanes)
-            )
-        for half, out in ((0, narrow_t), (1, narrow)):
-            out[:, 0, :, tp * part : (tp + 1) * part] = (
-                second[0, tp, half, 0].astype(F32).reshape(SETS, RANK, part)
-            )
+    for n in range(first.shape[2]):
+        for tp in range(first.shape[1]):
+            for half, target in ((0, up), (1, down_t)):
+                target[:, n, :, tp * lanes : (tp + 1) * lanes] = (
+                    first[0, tp, n, half].astype(F32).reshape(SETS, RANK, lanes)
+                )
+            for half, target in ((0, narrow_t), (1, narrow)):
+                target[:, n, :, tp * part : (tp + 1) * part] = (
+                    second[0, tp, half, n].astype(F32).reshape(SETS, RANK, part)
+                )
 
     @pl.when(pl.program_id(0) == 0)
     def _():
@@ -1211,23 +1238,27 @@
                 attend_up[:, p, :, k * 128 : (k + 1) * 128] = tile(late, p * count + k)
         for k in range(count):
             attend_down[:, :, k * 128 : (k + 1) * 128] = tile(late, 3 * count + k)
-        for p, out in enumerate((mixing_down, mixing_up, router_down)):
+        for p, target in enumerate((mixing_down, mixing_up, router_down)):
             for k in range(count):
-                out[:, :, k * 128 : (k + 1) * 128] = tile(early, p * count + k)
+                target[:, :, k * 128 : (k + 1) * 128] = tile(early, p * count + k)
         router_up[...] = tile(early, 3 * count)[:, :, :EXPERTS]
-
-
-def assemble(first, second, early, late):
+        out[...] = out_in[...]
+        grad[...] = grad_in[...]
+
+
+def assemble(first, second, early, late, out, grad):
     dp, tp, experts, _, width, lanes = first.shape
     part = second.shape[-1]
+    group = min(experts, ASSEMBLED)
+    groups = experts // group
 
     def split(e):
-        return lax.div(e, experts), lax.rem(e, experts)
+        return lax.div(e, groups), lax.rem(e, groups)
 
     def expert_out(size):
         return (
             jax.ShapeDtypeStruct((SETS, EXPERTS, RANK, size), F32),
-            pl.BlockSpec((SETS, 1, RANK, size), lambda e: (0, e, 0, 0)),
+            pl.BlockSpec((SETS, group, RANK, size), lambda e: (0, e, 0, 0)),
         )
 
     def whole_out(*shape):
@@ -1242,24 +1273,27 @@
         + [whole_out(SETS, RANK, D), whole_out(SETS, 3, RANK, D)]
         + [whole_out(SETS, RANK, D)] * 3
         + [whole_out(SETS, RANK, EXPERTS)]
+        + [(jax.ShapeDtypeStruct(out.shape, BF16), pl.BlockSpec(out.shape, lambda e: (0, 0, 0)))] * 2
     )
     return pl.pallas_call(
         assemble_kernel,
-        grid=(EXPERTS,),
+        grid=(EXPERTS // group,),
         out_shape=[out[0] for out in outs],
         in_specs=[
             pl.BlockSpec(
-                (1, tp, 1, 2, width, lanes), lambda e: (split(e)[0], 0, split(e)[1], 0, 0, 0)
+                (1, tp, group, 2, width, lanes), lambda e: (split(e)[0], 0, split(e)[1], 0, 0, 0)
             ),
             pl.BlockSpec(
-                (1, tp, 2, 1, width, part), lambda e: (split(e)[0], 0, 0, split(e)[1], 0, 0)
+                (1, tp, 2, group, width, part), lambda e: (split(e)[0], 0, 0, split(e)[1], 0, 0)
             ),
             pl.BlockSpec(early.shape, lambda e: (0, 0)),
             pl.BlockSpec(late.shape, lambda e: (0, 0)),
+            pl.BlockSpec(out.shape, lambda e: (0, 0, 0)),
+            pl.BlockSpec(grad.shape, lambda e: (0, 0, 0)),
         ],
         out_specs=[out[1] for out in outs],
-        compiler_params=pltpu.CompilerParams(vmem_limit_bytes=32 << 20),
-    )(first, second, early, late)
+        compiler_params=pltpu.CompilerParams(vmem_limit_bytes=60 << 20),
+    )(first, second, early, late, out, grad)
 
 
 def per_device(
@@ -1306,7 +1340,10 @@
         token_mask=token_mask,
         image_mask=image_mask,
         adapter_set=adapter_set,
-        gains=jnp.stack([first_gain, first_shift, second_gain, second_shift]),
+        first_gain=first_gain.reshape(1, D),
+        first_shift=first_shift.reshape(1, D),
+        second_gain=second_gain.reshape(1, D),
+        second_shift=second_shift.reshape(1, D),
         up_weight=expand_weight,
         down_weight=shrink_weight,
         attend_low=flipped(attend_down),
@@ -1325,10 +1362,12 @@
         made["second_all"],
         made["early_all"].reshape(-1, 128),
         made["late_all"].reshape(-1, 128),
-    )
-    return (
         made["out_all"],
         made["grad_all"],
+    )
+    return (
+        wide[10],
+        wide[11],
         flipped(wide[4]),
         jnp.transpose(wide[5], (0, 2, 1, 3)),
         flipped(wide[6]),

time: 206 us -> 180 us (0.87)
  Pallas kernels: 196 us -> 178 us
  local copies, waits for them, and re-layouts: 8.31 us -> 0 us
    pallas_call x1, Pallas kernels: 186 us -> 165 us  [run_layer(): pl.pallas_call(functools.partial(layer_kernel, sizes, names), out_shape=t...]
    unnamed x14 -> x0, local copies, waits for them, and re-layouts: 8.31 us -> none
    pallas_call x1, Pallas kernels: 10.1 us -> 13 us  [assemble(): pl.pallas_call(assemble_kernel, grid=(EXPERTS // group,), out_shape=[out[...]
where the time goes in v2:
time: 180 us; the launch traced here: 179 us
  Pallas kernels  178 us (99%)
    pallas_call x1, Pallas kernels, run_layer(): pl.pallas_call(functools.partial(layer_kernel, sizes, names), out_shape=t...  165 us
    pallas_call x1, Pallas kernels, assemble(): pl.pallas_call(assemble_kernel, grid=(EXPERTS // group,), out_shape=[out[...  13 us

profile of v2, /device:TPU:1, one launch (start us, length us, event | category | flops | bytes accessed | tf_op | source)
XLA Modules:
  0.0 179.3 jit_solution(2314994803803485370)
XLA Ops:
  0.7 165.5 %shard_map.337 = (bf16[4,2,4,2,64,1024]{5,4,3,2,1,0:T(8,128)(2,1)}, bf16[4,2,2,4,64,256]{5,4,3,2,1,0:T(8,128)(2,1)}, bf16[4,2,2,56,128]{4,3,2,1,0:T(8,128)(2,1)}...) custom-call(bf16[2,160,512]{2,1,0:T(8,128)(2,1)} %refs_0_.1, ...), custom_call_target="tpu_custom_call" | custom-call | tf_op jit(solution)/shard_map/pallas_call | solution.py:1200
  166.1 13.0 %shard_map.338 = (f32[4,16,16,2048]{3,2,1,0:T(8,128)}, f32[4,16,16,2048]{3,2,1,0:T(8,128)}, f32[4,16,16,512]{3,2,1,0:T(8,128)}, f32[4,16,16,512]{3,2,1,0:T(8,128...) custom-call(bf16[4,2,4,2,64,1024]{5,4,3,2,1,0:T(8,128)(2,1)} %get-tu, ...), custom_call_target="tpu_custom_call" | custom-call | tf_op jit(solution)/shard_map/pallas_call | solution.py:1278

commit v3 on v2

--- a/solution.py
+++ b/solution.py
@@ -23,7 +23,7 @@
 SET_ROW = LIVE_ROW + 1
 CRITICAL = D + 128
 EXPERT_ROWS = 256
-ASSEMBLED = 2
+ASSEMBLED = 4
 
 EPSILON = 1e-06
 MASKED = -1e30
@@ -654,6 +654,7 @@
         (r.early_sum, r.early_in, r.early_final, lambda dp, tp: r.early_all.at[dp, tp]),
         (r.late_sum, r.late_in, r.late_final, lambda dp, tp: r.late_all.at[dp, tp]),
     ]
+    second_at, early_at, late_at = experts, experts + 1, experts + 2
     inner, outer = place.inner, 1 - place.inner
     to_partner, to_far = {"ctx": place.partner}, {"ctx": place.far_mid}
     flows, spreads = [], []
@@ -668,7 +669,7 @@
                 away=wire.copy(final.at[inner], final.at[inner], {"ctx": place.far_end}),
             )
         )
-        spreads.append(Spread(place, wire, final, slot))
+        spreads.append(Spread(place, wire, final, slot, direct=len(spreads) >= early_at))
 
     def offer(k):
         @pl.when(place.is_end)
@@ -707,7 +708,6 @@
         total_half, settle, lambda k: spreads[k].forward(), lambda k: spreads[k].diagonal(),
     )
     reached = [0] * len(chunks)
-    second_at, early_at, late_at = experts, experts + 1, experts + 2
 
     def go(k, stage):
         while reached[k] < stage:
@@ -781,32 +781,31 @@
     second_swap = wire.copy(
         r.second.at[place.other_tp], r.second_got, {"tp": place.other_tp}
     )
-    swap = wire.copy(r.partial.at[1 - place.core], r.from_sibling, {"dp": place.sibling})
     second_swap.start()
-
-    def combine(core):
+    first_lanes, other_lanes = slice(0, CRITICAL), slice(CRITICAL, CRITICAL + D)
+    swaps = [
+        wire.copy(
+            r.partial.at[1 - place.core, :, :, :, at],
+            r.from_sibling.at[:, :, :, at],
+            {"dp": place.sibling},
+        )
+        for at in (first_lanes, other_lanes)
+    ]
+
+    def combine(core, at):
         def run(chip, _):
             for n in range(images):
                 i = (chip * 2 + core) * images + n
-                made = inner_rows(r.table[i], r.payload[i]).astype(BF16)
+                made = inner_rows(r.table[i], r.payload[i, :, at]).astype(BF16)
                 for t in range(place.tp_size):
-                    r.partial[core, chip, t, n * half : (n + 1) * half, :] = made[
+                    r.partial[core, chip, t, n * half : (n + 1) * half, at] = made[
                         t * half : (t + 1) * half
                     ]
             return 0
 
-        lax.fori_loop(0, place.chips, run, 0)
-
-    combine(1 - place.core)
-    swap.start()
-    combine(place.core)
-    at_point(2)
-    second_swap.wait()
-    r.second_sum[...] = add_rounded(r.second[place.tp], r.second_got[...])
-    offer(second_at)
-    swap.wait_recv()
-    returns = []
-    for at in (slice(0, CRITICAL), slice(CRITICAL, CRITICAL + D)):
+        lax.fori_loop(0, place.chips, run, 0, unroll=2)
+
+    def send_back(at):
         copies = []
         for i, j in place.offsets() + [(0, 0)]:
             dp, tp = place.ahead(i, j)
@@ -826,8 +825,23 @@
                 copies.append(copy)
             else:
                 r.received[0, :, at] = both
-        returns.append(copies)
-    late_sends = [swap] + returns[0] + returns[1]
+        return copies
+
+    combine(1 - place.core, first_lanes)
+    swaps[0].start()
+    combine(place.core, first_lanes)
+    at_point(2)
+    swaps[0].wait_recv()
+    returns = [send_back(first_lanes)]
+    combine(1 - place.core, other_lanes)
+    swaps[1].start()
+    combine(place.core, other_lanes)
+    second_swap.wait()
+    r.second_sum[...] = add_rounded(r.second[place.tp], r.second_got[...])
+    offer(second_at)
+    swaps[1].wait_recv()
+    returns.append(send_back(other_lanes))
+    late_sends = swaps + returns[0] + returns[1]
     at_point(3)
     for copy in returns[0]:
         copy.wait_recv()
@@ -1183,7 +1197,7 @@
         + (2 + images + chunks) * Spread.remote(sizes)
         + 3 * Spread.remote(sizes, False)
         + 6 * chunks
-        + 2
+        + 3
         + 2 * (chips * tp - 1)
         + 2 * (plane - 1)
         + 2

time: 180 us -> 177 us (0.983)
  Pallas kernels: 178 us -> 176 us
    pallas_call x1, Pallas kernels: 165 us -> 164 us  [run_layer(): pl.pallas_call(functools.partial(layer_kernel, sizes, names), out_shape=t...]
where the time goes in v3:
time: 177 us; the launch traced here: 176 us
  Pallas kernels  176 us (99%)
    pallas_call x1, Pallas kernels, run_layer(): pl.pallas_call(functools.partial(layer_kernel, sizes, names), out_shape=t...  164 us
    pallas_call x1, Pallas kernels, assemble(): pl.pallas_call(assemble_kernel, grid=(EXPERTS // group,), out_shape=[out[...  12 us

profile of v3, /device:TPU:1, one launch (start us, length us, event | category | flops | bytes accessed | tf_op | source)
XLA Modules:
  0.0 176.4 jit_solution(6619911725180264312)
XLA Ops:
  0.7 163.6 %shard_map.337 = (bf16[4,2,4,2,64,1024]{5,4,3,2,1,0:T(8,128)(2,1)}, bf16[4,2,2,4,64,256]{5,4,3,2,1,0:T(8,128)(2,1)}, bf16[4,2,2,56,128]{4,3,2,1,0:T(8,128)(2,1)}...) custom-call(bf16[2,160,512]{2,1,0:T(8,128)(2,1)} %refs_0_.1, ...), custom_call_target="tpu_custom_call" | custom-call | tf_op jit(solution)/shard_map/pallas_call | solution.py:1214
  164.2 12.0 %shard_map.338 = (f32[4,16,16,2048]{3,2,1,0:T(8,128)}, f32[4,16,16,2048]{3,2,1,0:T(8,128)}, f32[4,16,16,512]{3,2,1,0:T(8,128)}, f32[4,16,16,512]{3,2,1,0:T(8,128...) custom-call(bf16[4,2,4,2,64,1024]{5,4,3,2,1,0:T(8,128)(2,1)} %get-tu, ...), custom_call_target="tpu_custom_call" | custom-call | tf_op jit(solution)/shard_map/pallas_call | solution.py:1292

commit v4 on v3

--- a/solution.py
+++ b/solution.py
@@ -222,7 +222,10 @@
 
 
 class Spread:
-    def __init__(self, place, wire, source, slot, over_tp=True, direct=False, near=True):
+    def __init__(
+        self, place, wire, source, slot, over_tp=True, direct=False, near=True, turn=False
+    ):
+        self.turn = turn
         self.place, self.wire, self.source, self.slot = place, wire, source, slot
         self.over_tp = over_tp
         self.relay = over_tp and not direct and place.chips == 2 and place.tp_size == 2
@@ -253,8 +256,8 @@
         for copy, i, j in sorted(self.flights, key=lambda f: f[1]):
             copy.wait_recv()
             got = self.slot(*self.place.behind(i, j))
-            if self.relay and j:
-                dp, tp = self.place.ahead(1, 0)
+            if self.relay and (i if self.turn else j):
+                dp, tp = self.place.ahead(0, 1) if self.turn else self.place.ahead(1, 0)
                 self.across = self.wire.copy(got, got, {"dp": dp, "tp": tp})
                 self.across.start()
             self.to_sibling(got, got)
@@ -461,7 +464,6 @@
     numbers.start()
     router.start()
     mixing.start()
-    cotangents.start()
     wide = pl.ds(pl.multiple_of(place.tp * hidden_units, 128), hidden_units)
     for e in range(experts):
         load(("a_first", e), r.first_a.at[:, owned + e], r.v_first_a.at[e])
@@ -518,16 +520,11 @@
     tokens_chain.landed(1)
     mixing.forward()
     project_blocks(1, 2)
+    cotangents.start()
     tokens_chain.landed(2)
     project_blocks(2, 3)
-    cotangents.forward()
-    mixing.diagonal()
     tokens_chain.landed(3)
     project_blocks(3, 4)
-    mixing.finish()
-    need("mixing_low", "mixing_high")
-    mixing_low = r.v_mixing_low[...].reshape(WIDTH, D)
-    mixing_high = r.v_mixing_high[...].reshape(WIDTH, D)
 
     def open_keys(i):
         return (
@@ -567,6 +564,12 @@
             log = jnp.maximum(top + jnp.log(total), -1e29)
             logs += [log[:half], log[half:]]
         r.logs[part, :] = put_lanes(logs, 128)
+        if i == 0:
+            mixing.diagonal()
+            mixing.finish()
+            need("mixing_low", "mixing_high")
+            mixing_low = r.v_mixing_low[...].reshape(WIDTH, D)
+            mixing_high = r.v_mixing_high[...].reshape(WIDTH, D)
         mix = r.head_mix[part, :]
         lift = (times_transposed(mix, mixing_low) * picks[i]).astype(BF16)
         r.mixing_lift[part, :] = lift
@@ -579,6 +582,7 @@
         expert_rows[i].start()
 
     slots = experts * SLOTS
+    cotangents.forward()
     cotangents.finish()
     numbers.finish()
     router.finish()
@@ -669,7 +673,10 @@
                 away=wire.copy(final.at[inner], final.at[inner], {"ctx": place.far_end}),
             )
         )
-        spreads.append(Spread(place, wire, final, slot, direct=len(spreads) >= early_at))
+        k = len(spreads)
+        spreads.append(
+            Spread(place, wire, final, slot, direct=k >= early_at, turn=k == second_at)
+        )
 
     def offer(k):
         @pl.when(place.is_end)

time: 177 us -> 170 us (0.960)
  Pallas kernels: 176 us -> 169 us
    pallas_call x1, Pallas kernels: 164 us -> 157 us  [run_layer(): pl.pallas_call(functools.partial(layer_kernel, sizes, names), out_shape=t...]
where the time goes in v4:
time: 170 us
  Pallas kernels  169 us (99%)
    pallas_call x1, Pallas kernels, run_layer(): pl.pallas_call(functools.partial(layer_kernel, sizes, names), out_shape=t...  157 us
    pallas_call x1, Pallas kernels, assemble(): pl.pallas_call(assemble_kernel, grid=(EXPERTS // group,), out_shape=[out[...  12 us

profile of v4, /device:TPU:1, one launch (start us, length us, event | category | flops | bytes accessed | tf_op | source)
XLA Modules:
  0.0 169.7 jit_solution(7496852109607679481)
XLA Ops:
  0.7 156.8 %shard_map.337 = (bf16[4,2,4,2,64,1024]{5,4,3,2,1,0:T(8,128)(2,1)}, bf16[4,2,2,4,64,256]{5,4,3,2,1,0:T(8,128)(2,1)}, bf16[4,2,2,56,128]{4,3,2,1,0:T(8,128)(2,1)}...) custom-call(bf16[2,160,512]{2,1,0:T(8,128)(2,1)} %refs_0_.1, ...), custom_call_target="tpu_custom_call" | custom-call | tf_op jit(solution)/shard_map/pallas_call | solution.py:1221
  157.5 12.0 %shard_map.338 = (f32[4,16,16,2048]{3,2,1,0:T(8,128)}, f32[4,16,16,2048]{3,2,1,0:T(8,128)}, f32[4,16,16,512]{3,2,1,0:T(8,128)}, f32[4,16,16,512]{3,2,1,0:T(8,128...) custom-call(bf16[4,2,4,2,64,1024]{5,4,3,2,1,0:T(8,128)(2,1)} %get-tu, ...), custom_call_target="tpu_custom_call" | custom-call | tf_op jit(solution)/shard_map/pallas_call | solution.py:1299

commit v5 on v4

--- a/solution.py
+++ b/solution.py
@@ -125,7 +125,7 @@
     ((SECOND, ONWARD),),
     ((EARLY, SENT),),
     (
-        (E3, DONE), (LATE, SUM), (EARLY, ONWARD), (SECOND, DONE), (LATE, SENT), (EARLY, DONE),
+        (LATE, SUM), (E3, DONE), (EARLY, ONWARD), (LATE, SENT), (SECOND, DONE), (EARLY, DONE),
         (LATE, ONWARD), (LATE, DONE),
     ),
 )
@@ -613,7 +613,7 @@
         fill_slots(i, r.grad_slots, matmul(hot, r.cot_all[i]).astype(BF16))
         return 0
 
-    lax.fori_loop(0, all_images, make_table, 0, unroll=2)
+    lax.fori_loop(0, all_images, make_table, 0, unroll=4)
     for spread in expert_rows:
         spread.forward()
     for spread in expert_rows:
@@ -644,7 +644,7 @@
         r.slot_sets[at, :] = (lane == given[SET_ROW : SET_ROW + 1, 0:1]).astype(F32)
         return 0
 
-    lax.fori_loop(0, all_images, dispatch, 0, unroll=4)
+    lax.fori_loop(0, all_images, dispatch, 0, unroll=8)
 
     chunks = [
         (

time: 170 us -> 170 us (level)
  no operation moved by 1% of the time
where the time goes in v5:
time: 170 us
  Pallas kernels  169 us (99%)
    pallas_call x1, Pallas kernels, run_layer(): pl.pallas_call(functools.partial(layer_kernel, sizes, names), out_shape=t...  157 us
    pallas_call x1, Pallas kernels, assemble(): pl.pallas_call(assemble_kernel, grid=(EXPERTS // group,), out_shape=[out[...  12 us

profile of v5, /device:TPU:1, one launch (start us, length us, event | category | flops | bytes accessed | tf_op | source)
XLA Modules:
  0.0 169.7 jit_solution(5534140846457617302)
XLA Ops:
  0.7 156.9 %shard_map.337 = (bf16[4,2,4,2,64,1024]{5,4,3,2,1,0:T(8,128)(2,1)}, bf16[4,2,2,4,64,256]{5,4,3,2,1,0:T(8,128)(2,1)}, bf16[4,2,2,56,128]{4,3,2,1,0:T(8,128)(2,1)}...) custom-call(bf16[2,160,512]{2,1,0:T(8,128)(2,1)} %refs_0_.1, ...), custom_call_target="tpu_custom_call" | custom-call | tf_op jit(solution)/shard_map/pallas_call | solution.py:1221
  157.6 12.0 %shard_map.338 = (f32[4,16,16,2048]{3,2,1,0:T(8,128)}, f32[4,16,16,2048]{3,2,1,0:T(8,128)}, f32[4,16,16,512]{3,2,1,0:T(8,128)}, f32[4,16,16,512]{3,2,1,0:T(8,128...) custom-call(bf16[4,2,4,2,64,1024]{5,4,3,2,1,0:T(8,128)(2,1)} %get-tu, ...), custom_call_target="tpu_custom_call" | custom-call | tf_op jit(solution)/shard_map/pallas_call | solution.py:1299
